TPU v7x, 32 devices: a whole 2x2x4 slice. The times are simulated.
32 devices in a mesh: tile: 16 (over z, y, x), vec: 2 (over core).
Axes of the slice: x: 2, y: 2, z: 4, core: 2. Of those that a mesh axis runs over, the one named last changes fastest.
Arguments:
- trial: bfloat16 [1, 1024, 1024], P(None, ('tile', 'vec')), may hold values from -0.005859375 to 0.005859375
- psi_v: bfloat16 [1024, 8192], P(None, 'tile'), may hold values from -6 to 6
- psi_c: bfloat16 [1024, 2, 4096], P(None, 'vec', 'tile'), may hold values from -6 to 6
- screened: float32 [8192, 8192], P('tile', 'vec'), may hold values from -0.0007324219 to 0.0007324219
Outputs:
- result: float32 [1, 1024, 1024], P(None, ('tile', 'vec'))
All inputs are finite; a program needn't handle non-finite values.
Results may differ from a plain program's by a relative error of at most 0.0041.
Values may be sent and summed in bfloat16 or wider, within the bound.
A program may use at most 64 MiB of HBM per device.

v0:
```python
import functools

import jax
import jax.numpy as jnp
from jax import lax
from jax.experimental import pallas as pl
from jax.experimental.pallas import tpu as pltpu
from jax.sharding import PartitionSpec as P

RING = 4
CUTS = 4
EARLY = 3


def back_product(weighted_flat, panel):
    return lax.dot_general(
        weighted_flat, panel, (((1,), (1,)), ((), ())), preferred_element_type=jnp.float32
    )


def plain(trial, psi_v, psi_c, screened):
    count = trial.shape[0]
    points = psi_v.shape[1]
    conduct = trial.shape[2]
    whole = lax.all_gather(trial, ("tile", "vec"), axis=1, tiled=True)
    projected = jnp.einsum("vp,kvc->kpc", psi_v, whole, preferred_element_type=jnp.float32).astype(
        jnp.bfloat16
    )
    flat = projected.reshape(count * points, conduct)
    panel_local = psi_c[:, 0, :]
    panel = lax.all_gather(panel_local, "tile", axis=1, tiled=True)
    pair = jnp.dot(flat, panel, preferred_element_type=jnp.float32)
    weighted = (screened[None] * pair.reshape(count, points, -1)).astype(jnp.bfloat16)
    weighted_flat = weighted.reshape(count * points, -1)
    back = back_product(weighted_flat, panel)
    back = back.reshape(count, points, conduct)
    left = psi_v.astype(jnp.float32)
    summed = lax.psum(back, "vec")
    tiles = lax.axis_size("tile")
    halves = lax.axis_size("vec")
    owned = left.shape[0] // (tiles * halves)
    grouped = left.reshape(tiles, halves, owned, points)
    mine = lax.dynamic_index_in_dim(grouped, lax.axis_index("vec"), 1, keepdims=False).reshape(
        tiles * owned, points
    )
    pieces = []
    for one in range(count):
        term = jnp.dot(mine, summed[one], precision=lax.Precision.HIGHEST)
        pieces.append(lax.psum_scatter(term, "tile", scatter_dimension=0, tiled=True))
    return jnp.stack(pieces, axis=0)


def gray(r):
    return r + (r // 2) - 2 * (r // 3)


def flip_bits(a, mask):
    bit = 1
    while bit <= mask:
        if mask & bit:
            a = a + bit - 2 * bit * ((a // bit) % 2)
        bit *= 2
    return a


def arrivals(layers):
    near = [d for d in [1] + list(range(layers - 1, 1, -1)) if d < layers]
    order = [(0, 0)]
    order += [(d, 0) for d in near[:1]]
    order += [(0, 1), (0, 3)]
    for d in near[:1]:
        order += [(d, 3), (d, 1)]
    order += [(d, 0) for d in near[1:2]]
    order += [(0, 2)]
    order += [(d, 0) for d in near[2:]]
    for d in near[1:]:
        order += [(d, 3), (d, 1)]
    order += [(d, 2) for d in near]
    return near, order


def body(
    tiles,
    trial_ref,
    psi_v_hbm,
    psi_c_ref,
    screened_hbm,
    out_ref,
    whole,
    psi_v,
    psi_t,
    screened,
    panel,
    flat,
    back,
    give,
    take,
    term,
    parts,
    local_sem,
    trial_send,
    trial_recv,
    hand_send,
    hand_recv,
    block_send,
    block_recv,
    back_sem,
    part_send,
    part_recv,
):
    layers = tiles // RING
    me = lax.axis_index("tile")
    half = lax.axis_index("vec")
    other = 1 - half
    a = me // RING
    r = gray(me % RING)
    near, order = arrivals(layers)
    slot = {event: i for i, event in enumerate(order)}

    def at(da, dr):
        return flip_bits(a, da) * RING + gray((r + dr) % RING)

    columns_of = {d: at(d, 0) for d in range(1, layers)}
    ahead, behind = at(0, 1), at(0, RING - 1)

    def remote(src, dst, send, recv, tile, vec):
        return pltpu.make_async_remote_copy(
            src_ref=src,
            dst_ref=dst,
            send_sem=send,
            recv_sem=recv,
            device_id=(tile, vec),
            device_id_type=pl.DeviceIdType.MESH,
        )

    load_psi = pltpu.make_async_copy(psi_v_hbm, psi_v, local_sem.at[0])
    load_psi.start()
    load_screened = pltpu.make_async_copy(screened_hbm, screened, local_sem.at[1])
    load_screened.start()

    barrier = pltpu.get_barrier_semaphore()
    for d in range(1, tiles):
        for v in range(2):
            pl.semaphore_signal(
                barrier,
                inc=1,
                device_id=((me + d) % tiles, v),
                device_id_type=pl.DeviceIdType.MESH,
            )
    pl.semaphore_signal(
        barrier, inc=1, device_id=(me, other), device_id_type=pl.DeviceIdType.MESH
    )
    pl.semaphore_wait(barrier, 2 * tiles - 1)

    rows = trial_ref.shape[0]

    def lines(tile, vec):
        start = pl.multiple_of((tile * 2 + vec) * rows, rows)
        return whole.at[pl.ds(start, rows), :]

    def owner_of(event):
        da, dr = event
        return at(da, (RING - dr) % RING)

    owners = {event: owner_of(event) for event in order}

    def targets(event):
        da, dr = event
        if event == (0, 0):
            return [((0, 1), ahead), ((0, 3), behind)] + [((d, 0), at(d, 0)) for d in near]
        if dr == 0:
            return [((da, 1), ahead), ((da, 3), behind)]
        if dr == 1 and da % 2 == 0:
            return [((da, 2), ahead)]
        if dr == 3 and da % 2 == 1:
            return [((da, 2), behind)]
        return []

    sent = []

    def pass_on(event, src):
        owner = owners[event]
        d = slot[event]
        for later, tile in targets(event):
            i = slot[later]
            copy = remote(src, lines(owner, half), trial_send.at[i], trial_recv.at[i], tile, half)
            copy.start()
            sent.append(copy)
        copy = remote(src, lines(owner, half), hand_send.at[d], hand_recv.at[d], me, other)
        copy.start()
        sent.append(copy)

    def take_rows(event):
        ref = lines(owners[event], half)
        remote(ref, ref, trial_send.at[0], trial_recv.at[slot[event]], me, other).wait_recv()
        pass_on(event, ref)

    pass_on((0, 0), trial_ref)

    height = psi_c_ref.shape[0] // CUTS
    counter = [0]

    def piece(ref, s):
        return ref.at[pl.ds(s * height, height), :]

    def send_block(event, s, src, owner, tile):
        copy = remote(
            piece(src, s),
            piece(panel.at[owner], s),
            block_send.at[counter[0]],
            block_recv.at[slot[event], s],
            tile,
            half,
        )
        counter[0] += 1
        copy.start()

    for d in near:
        for s in range(CUTS):
            send_block((d, 0), s, psi_c_ref, me, at(d, 0))

    def arrive(event):
        owner = owners[event]
        for s in range(CUTS):
            ref = piece(panel.at[owner], s)
            remote(
                ref, ref, block_send.at[0], block_recv.at[slot[event], s], me, other
            ).wait_recv()
            onward = targets(event)
            if s == CUTS - 1 and event == (0, 2):
                onward = [((d, 2), columns_of[d]) for d in near]
            elif s == CUTS - 1 and event[0] != 0 and event[1] != 0:
                onward = []
            for later, tile in onward:
                send_block(later, s, panel.at[owner], owner, tile)

    early = min(EARLY, len(order) - 1)
    for d in near:
        take_rows((d, 0))
    for s in range(CUTS):
        send_block((0, 1), s, psi_c_ref, me, ahead)
        send_block((0, 3), s, psi_c_ref, me, behind)
    whole[pl.ds(pl.multiple_of((me * 2 + half) * rows, rows), rows), :] = trial_ref[...]
    panel[pl.ds(me, 1)] = psi_c_ref[...][None]
    back[...] = jnp.zeros_like(back)
    load_psi.wait()
    psi_t[...] = psi_v[...].T

    for event in order[1:]:
        if event[1] in (1, 3):
            take_rows(event)
    for event in order[1 : early + 1]:
        arrive(event)
    for event in order[1:]:
        if event[1] == 2:
            take_rows(event)
    for event in order:
        ref = lines(owners[event], other)
        remote(ref, ref, hand_send.at[0], hand_recv.at[slot[event]], me, other).wait_recv()

    conduct = whole.shape[1]
    wide = 256

    def project(j, carry):
        columns = pl.ds(pl.multiple_of(j * wide, wide), wide)
        flat[:, columns] = jnp.dot(
            psi_t[...], whole[:, columns], preferred_element_type=jnp.float32
        ).astype(jnp.bfloat16)
        return carry

    lax.fori_loop(0, conduct // wide, project, 0)
    load_screened.wait()

    width = psi_c_ref.shape[1]
    middle = conduct // 2

    def use(k, carry):
        owner = me
        for i, event in enumerate(order):
            if i > early:

                @pl.when(k == i)
                def _(event=event):
                    arrive(event)

            owner = jnp.where(k == i, owners[event], owner)
        block = panel.at[owner]
        pair = jnp.dot(flat[...], block[...], preferred_element_type=jnp.float32)
        columns = pl.ds(pl.multiple_of(owner * width, 128), width)
        weighted = (screened[:, columns] * pair).astype(jnp.bfloat16)
        for h in range(2):
            back[h] += back_product(weighted, block[pl.ds(h * middle, middle), :])
        return carry

    lax.fori_loop(0, tiles, use, 0)

    give[...] = back[other].astype(jnp.bfloat16)
    swap = remote(give, take, back_sem.at[0], back_sem.at[1], me, other)
    swap.start()
    swap.wait()
    total = back[half] + take[...].astype(jnp.float32)
    high = total.astype(jnp.bfloat16)
    low = (total - high.astype(jnp.float32)).astype(jnp.bfloat16)
    flat[:, :middle] = high
    flat[:, middle:] = low
    span = 2 * rows
    step = psi_v.shape[0] // 4

    def finish(j, carry):
        lines_of = pl.ds(pl.multiple_of(j * step, step), step)
        left = psi_v[lines_of, :]
        term[lines_of, :] = (
            jnp.dot(left, flat[:, :middle], preferred_element_type=jnp.float32)
            + jnp.dot(left, flat[:, middle:], preferred_element_type=jnp.float32)
        ).astype(jnp.bfloat16)
        return carry

    lax.fori_loop(0, 4, finish, 0)

    def owned(tile, vec):
        return pl.ds(pl.multiple_of(tile * span + vec * rows, rows), rows)

    for d in list(range(1, tiles)) + [0]:
        for flip in range(2):
            if d == 0 and flip == 0:
                continue
            tile = (me + d) % tiles
            vec = (half + flip) % 2
            copy = remote(
                term.at[owned(tile, vec), :],
                parts.at[me, half],
                part_send.at[d, flip],
                part_recv.at[d, flip],
                tile,
                vec,
            )
            copy.start()
            sent.append(copy)
    sums = [term[owned(me, half), :].astype(jnp.float32), None]
    for d in [0] + list(range(1, tiles)):
        for flip in range(2):
            if d == 0 and flip == 0:
                continue
            ref = parts.at[(me + tiles - d) % tiles, (half + flip) % 2]
            remote(ref, ref, part_send.at[0, 0], part_recv.at[d, flip], me, other).wait_recv()
            value = ref[...].astype(jnp.float32)
            sums[flip] = value if sums[flip] is None else sums[flip] + value
    for flip in range(2):
        place = (half + flip) % 2
        out_ref[:, pl.ds(pl.multiple_of(place * middle, 128), middle)] = sums[flip]
    for copy in sent:
        copy.wait_send()
    for i in range(counter[0]):
        ref = piece(psi_c_ref, 0)
        remote(ref, ref, block_send.at[i], block_recv.at[0, 0], me, other).wait_send()


def fused(tiles, trial, psi_v, psi_c, screened):
    rows, conduct = trial.shape[1:]
    valence, points = psi_v.shape
    width = psi_c.shape[2]
    middle = conduct // 2
    bf16, f32 = jnp.bfloat16, jnp.float32
    vmem = pl.BlockSpec(memory_space=pltpu.VMEM)
    far = pl.BlockSpec(memory_space=pl.ANY)
    dma = pltpu.SemaphoreType.DMA
    out = pl.pallas_call(
        functools.partial(body, tiles),
        out_shape=jax.ShapeDtypeStruct((rows, conduct), f32),
        in_specs=[vmem, far, vmem, far],
        out_specs=vmem,
        scratch_shapes=[
            pltpu.VMEM((valence, conduct), bf16),
            pltpu.VMEM((valence, points), bf16),
            pltpu.VMEM((points, valence), bf16),
            pltpu.VMEM(screened.shape, f32),
            pltpu.VMEM((tiles, conduct, width), bf16),
            pltpu.VMEM((points, conduct), bf16),
            pltpu.VMEM((2, points, middle), f32),
            pltpu.VMEM((points, middle), bf16),
            pltpu.VMEM((points, middle), bf16),
            pltpu.VMEM((valence, middle), bf16),
            pltpu.VMEM((tiles, 2, rows, middle), bf16),
            dma((2,)),
            dma((tiles,)),
            dma((tiles,)),
            dma((tiles,)),
            dma((tiles,)),
            dma((tiles * CUTS,)),
            dma((tiles, CUTS)),
            dma((2,)),
            dma((tiles, 2)),
            dma((tiles, 2)),
        ],
        compiler_params=pltpu.CompilerParams(
            collective_id=0, has_side_effects=True, vmem_limit_bytes=58 * 1024 * 1024
        ),
    )(trial[0], psi_v, psi_c[:, 0, :], screened)
    return out[None]


def solution(mesh):
    tiles = mesh.shape["tile"]

    def shards(trial, psi_v, psi_c, screened):
        fits = (
            trial.shape[0] == 1
            and mesh.shape["vec"] == 2
            and tiles % RING == 0
            and (tiles & (tiles - 1)) == 0
            and psi_c.shape[2] % 128 == 0
            and trial.shape[1] % 16 == 0
            and trial.shape[2] % 256 == 0
        )
        if fits:
            return fused(tiles, trial, psi_v, psi_c, screened)
        return plain(trial, psi_v, psi_c, screened)

    in_specs = (
        P(None, ("tile", "vec"), None),
        P(None, "tile"),
        P(None, "vec", "tile"),
        P("tile", "vec"),
    )
    out_specs = P(None, ("tile", "vec"), None)
    return jax.shard_map(shards, mesh=mesh, in_specs=in_specs, out_specs=out_specs, check_vma=False)
```

profile of v0, /device:TPU:15, one launch (start us, length us, event | category | flops | bytes accessed | tf_op | source)
XLA Modules:
  0.0 118.3 jit_solution(16201588724485348818)
XLA Ops:
  0.0 116.7 %shard_map.46 = f32[32,1024]{1,0:T(8,128)} custom-call(bf16[32,1024]{1,0:T(8,128)(2,1)} %bitcast.5, bf16[1024,512]{1,0:T(8,128)(2,1)} %psi_v_hbm.1, bf16[1024,256]{1,0:T(8,128)(2,1)} %bitcast.4, f32[512,4096]{1,0:T(8,128)} %screened_hbm.1), custom_call_target="tpu_custom_call" | custom-call | tf_op jit(solution)/shard_map/pallas_call | solution.py:367
  116.7 1.6 %copy.6 = f32[1,32,1024]{2,1,0:T(8,128)} copy(f32[1,32,1024]{2,1,0:T(8,128)} %bitcast.3) | data formatting | bytes 262144
where the time goes:
time: 118 us
  Pallas kernels  117 us (99%)
  local copies, waits for them, and re-layouts  1.57 us (1%)
    pallas_call x1, Pallas kernels, fused(): pl.pallas_call(functools.partial(body, tiles), out_shape=jax.ShapeDtypeSt...  117 us

commit v1 on v0

v1 whole, which is shorter than its diff:
```python
import functools

import jax
import jax.numpy as jnp
from jax import lax
from jax.experimental import pallas as pl
from jax.experimental.pallas import tpu as pltpu
from jax.sharding import PartitionSpec as P

CUTS = 4
SUBS = 2


def back_product(weighted_flat, panel):
    return lax.dot_general(
        weighted_flat, panel, (((1,), (1,)), ((), ())), preferred_element_type=jnp.float32
    )


def plain(trial, psi_v, psi_c, screened):
    count = trial.shape[0]
    points = psi_v.shape[1]
    conduct = trial.shape[2]
    whole = lax.all_gather(trial, ("tile", "vec"), axis=1, tiled=True)
    projected = jnp.einsum("vp,kvc->kpc", psi_v, whole, preferred_element_type=jnp.float32).astype(
        jnp.bfloat16
    )
    flat = projected.reshape(count * points, conduct)
    panel_local = psi_c[:, 0, :]
    panel = lax.all_gather(panel_local, "tile", axis=1, tiled=True)
    pair = jnp.dot(flat, panel, preferred_element_type=jnp.float32)
    weighted = (screened[None] * pair.reshape(count, points, -1)).astype(jnp.bfloat16)
    weighted_flat = weighted.reshape(count * points, -1)
    back = back_product(weighted_flat, panel)
    back = back.reshape(count, points, conduct)
    left = psi_v.astype(jnp.float32)
    summed = lax.psum(back, "vec")
    tiles = lax.axis_size("tile")
    halves = lax.axis_size("vec")
    owned = left.shape[0] // (tiles * halves)
    grouped = left.reshape(tiles, halves, owned, points)
    mine = lax.dynamic_index_in_dim(grouped, lax.axis_index("vec"), 1, keepdims=False).reshape(
        tiles * owned, points
    )
    pieces = []
    for one in range(count):
        term = jnp.dot(mine, summed[one], precision=lax.Precision.HIGHEST)
        pieces.append(lax.psum_scatter(term, "tile", scatter_dimension=0, tiled=True))
    return jnp.stack(pieces, axis=0)


def sources_of(layers):
    return [
        sorted((o for o in range(layers) if o != z), key=lambda o: (abs(o - z), o))
        for z in range(layers)
    ]


def pick(values, at):
    chosen = jnp.int32(values[0])
    for k, value in enumerate(values[1:], 1):
        chosen = jnp.where(at == k, jnp.int32(value), chosen)
    return chosen


def body(
    layers,
    trial_hbm,
    psi_v_hbm,
    psi_c_hbm,
    screened_hbm,
    out_ref,
    whole,
    psi,
    psi_t,
    stage,
    screened_own,
    screened_out,
    screened_in,
    panel,
    flat,
    back,
    give,
    take,
    first_send,
    first_got,
    keep,
    second_send,
    second_got,
    third,
    parts,
    local_sem,
    sends,
    trial_recv,
    hand_recv,
    psi_recv,
    screened_recv,
    block_recv,
    take_recv,
    first_recv,
    second_recv,
    parts_recv,
):
    bf16, f32 = jnp.bfloat16, jnp.float32
    me = lax.axis_index("tile")
    half = lax.axis_index("vec")
    other = 1 - half
    z, y, x = me // 4, (me // 2) % 2, me % 2
    across = lax.rem(y + 1, 2)
    aside = lax.rem(x + 1, 2)
    table = sources_of(layers)
    events = layers - 1
    source = [pick([row[e] for row in table], z) for e in range(events)]
    distance = [pick([abs(row[e] - k) for k, row in enumerate(table)], z) for e in range(events)]
    at_distance = [[distance[e] == k for k in range(layers)] for e in range(events)]

    def tile_of(zz, yy, xx):
        return zz * 4 + yy * 2 + xx

    mate_x, mate_y = tile_of(z, y, aside), tile_of(z, across, x)
    up, down = jnp.minimum(z + 1, layers - 1), jnp.maximum(z - 1, 0)
    has_up, has_down = z < layers - 1, z > 0
    on_up = [has_up & (source[e] < z) for e in range(events)]
    on_down = [has_down & (source[e] > z) for e in range(events)]

    def slot_of(zz, yy):
        return zz * 2 + yy

    slots = layers * 2
    order = [("own", 0)]
    for e in range(events):
        order += [("z", e), ("y", e - 1)]
    order += [("y", events - 1)]

    def slot_at(kind, e):
        zz = source[e] if e >= 0 and kind != "own" else z
        return slot_of(zz, across if kind == "y" else y)

    turns = [slot_at(*event) for event in order]

    rows, conduct = trial_hbm.shape
    width = psi_c_hbm.shape[1]
    points = psi_v_hbm.shape[-1]
    middle = conduct // 2
    part = middle // 2
    height = psi_c_hbm.shape[0] // CUTS

    def lines(tile, vec):
        start = pl.multiple_of((tile * 2 + vec) * rows, rows)
        return whole.at[pl.ds(start, rows), :]

    def columns(tile):
        return pl.ds(pl.multiple_of(tile * width, 128), width)

    local = []

    def load(src, dst):
        copy = pltpu.make_async_copy(src, dst, local_sem.at[len(local)])
        copy.start()
        local.append(copy)
        return copy

    load_psi = load(psi_v_hbm, psi.at[0])
    load_rows = load(trial_hbm, lines(me, half))
    load_out = [
        load(screened_hbm.at[:, columns(turn * 2 + aside)], stage.at[i])
        for i, turn in enumerate(turns)
    ]
    load_block = load(psi_c_hbm, panel.at[slot_of(z, y)])
    load_own = [
        load(screened_hbm.at[:, columns(turn * 2 + x)], screened_own.at[i])
        for i, turn in enumerate(turns)
    ]

    def remote(src, dst, send, recv, tile, vec):
        return pltpu.make_async_remote_copy(
            src_ref=src,
            dst_ref=dst,
            send_sem=send,
            recv_sem=recv,
            device_id=(tile, vec),
            device_id_type=pl.DeviceIdType.MESH,
        )

    partners = [(mate_x, half), (mate_y, half), (me, other)]
    for d in range(1, layers):
        for v in range(2):
            partners.append((tile_of(lax.rem(z + d, layers), y, x), v))
    with jax.named_scope("pbar"):
        barrier = pltpu.get_barrier_semaphore()
        for partner in partners:
            pl.semaphore_signal(
                barrier, inc=1, device_id=partner, device_id_type=pl.DeviceIdType.MESH
            )
        pl.semaphore_wait(barrier, len(partners))

    pending = []

    def send(src, dst, recv, tile, vec, like, cond=None):
        i = len(pending)
        copy = remote(src, dst, sends.at[i], recv, tile, vec)
        pending.append((like, cond))
        if cond is None:
            copy.start()
        else:
            pl.when(cond)(copy.start)

    def got(ref, recv):
        remote(ref, ref, sends.at[0], recv, me, other).wait_recv()

    some_rows = whole.at[pl.ds(0, rows), :]

    def piece(ref, s):
        return ref.at[pl.ds(s * height, height), :]

    some_piece = piece(panel.at[0], 0)

    def hand(src, tile):
        send(src, lines(tile, half), hand_recv.at[tile], me, other, some_rows)

    def spread(src, tile, to_up, to_down):
        dst = lines(tile, half)
        recv = trial_recv.at[tile]
        send(src, dst, recv, tile_of(up, y, x), half, some_rows, to_up)
        send(src, dst, recv, tile_of(down, y, x), half, some_rows, to_down)
        send(src, dst, recv, mate_y, half, some_rows)
        hand(src, tile)

    def own_piece(s):
        src = piece(psi_c_hbm, s)
        slot = slot_of(z, y)
        dst = piece(panel.at[slot], s)
        recv = block_recv.at[slot, s]
        send(src, dst, recv, tile_of(up, y, x), half, some_piece, has_up)
        send(src, dst, recv, tile_of(down, y, x), half, some_piece, has_down)
        send(src, dst, recv, mate_y, half, some_piece)

    pair_layers = layers // 2

    def psi_half(ref, which):
        return ref.at[pl.ds(which * pair_layers, pair_layers)]

    with jax.named_scope("ptrial"):
        send(trial_hbm, lines(me, half), trial_recv.at[me], mate_x, half, some_rows)
        spread(trial_hbm, me, has_up, has_down)
        own_piece(0)
        send(
            psi_half(psi_v_hbm, half),
            psi_half(psi.at[1], half),
            psi_recv.at[0],
            mate_x,
            half,
            psi_half(psi.at[1], 0),
        )
        got(lines(mate_x, half), trial_recv.at[mate_x])
        spread(lines(mate_x, half), mate_x, has_up, has_down)

        for i in range(slots):
            load_out[i].wait()
            screened_out[i] = stage[i].astype(bf16)
        for i in range(slots):
            send(
                screened_out.at[i],
                screened_in.at[i],
                screened_recv.at[i],
                mate_x,
                half,
                screened_out.at[0],
            )

        for e in range(events):
            for xx in range(2):
                tile = tile_of(source[e], y, xx)
                ref = lines(tile, half)
                got(ref, trial_recv.at[tile])
                spread(ref, tile, on_up[e], on_down[e])
            if e + 1 < CUTS:
                own_piece(e + 1)
        for s in range(events + 1, CUTS):
            own_piece(s)

        back[...] = jnp.zeros_like(back)
        load_psi.wait()
        valence = layers * 4 * 2 * rows
        psi_t[0] = psi[0].reshape(valence, points).T

        for e in range(-1, events):
            for xx in range(2):
                tile = tile_of(source[e] if e >= 0 else z, across, xx)
                ref = lines(tile, half)
                got(ref, trial_recv.at[tile])
                hand(ref, tile)

        ref = psi_half(psi.at[1], half)
        got(ref, psi_recv.at[0])
        send(ref, ref, psi_recv.at[1], me, other, psi_half(psi.at[1], 0))
        load_rows.wait()
        for tile in range(layers * 4):
            got(lines(tile, other), hand_recv.at[tile])

    wide = 256

    def project(p):
        def chunk(j, carry):
            cols = pl.ds(pl.multiple_of(j * wide, wide), wide)
            flat[p, :, cols] = jnp.dot(
                psi_t[p], whole[:, cols], preferred_element_type=f32
            ).astype(bf16)
            return carry

        lax.fori_loop(0, conduct // wide, chunk, 0)

    with jax.named_scope("pproj"):
        project(0)
        got(psi_half(psi.at[1], other), psi_recv.at[1])
        psi_t[1] = psi[1].reshape(valence, points).T
        project(1)

    def arrive(e):
        slot = slot_of(source[e], y)
        for s in range(CUTS):
            ref = piece(panel.at[slot], s)
            recv = block_recv.at[slot, s]
            got(ref, recv)
            send(ref, ref, recv, mate_y, half, some_piece, None)
            send(ref, ref, recv, tile_of(up, y, x), half, some_piece, on_up[e])
            send(ref, ref, recv, tile_of(down, y, x), half, some_piece, on_down[e])

    def arrive_if(e, k):
        start = len(pending)

        @pl.when(at_distance[e][k])
        def _():
            arrive(e)

        for i in range(start, len(pending)):
            pending[i] += (at_distance[e][k],)

    def receive(i):
        kind, e = order[i]
        if kind == "z":
            for late in range(e, events):
                arrive_if(late, e + 1)
        if kind == "y":
            slot = turns[i]
            for s in range(CUTS):
                got(piece(panel.at[slot], s), block_recv.at[slot, s])
        load_own[i].wait()

    def step(p, share, slot):
        block = panel.at[slot]
        pair = jnp.dot(flat[p], block[...], preferred_element_type=f32)
        weighted = (share.astype(f32) * pair).astype(bf16)
        for h in range(2):
            back[p, h] += back_product(weighted, block[pl.ds(h * middle, middle), :])

    load_block.wait()

    def use(k, carry):
        slot = turns[0]
        for i in range(slots):
            slot = jnp.where(k == i, turns[i], slot)

            @pl.when(k == i)
            def _(i=i):
                receive(i)

        step(0, screened_own[k], slot)
        got(screened_in.at[k], screened_recv.at[k])
        step(1, screened_in[k], slot)
        return carry

    with jax.named_scope("puse"):
        lax.fori_loop(0, slots, use, 0)

    def span(kind):
        return pl.ds(kind * part, part)

    with jax.named_scope("pswap"):
        for kind in range(2):
            for p in range(2):
                give[kind, p] = back[p, other, :, span(kind)].astype(bf16)
                send(
                    give.at[kind, p],
                    take.at[kind, p],
                    take_recv.at[kind, p],
                    me,
                    other,
                    give.at[0, 0],
                )

    share = layers // SUBS
    block_rows = 2 * rows

    def product(kind, at, sub):
        total = None
        for p in range(2):
            if kind == 0:
                left = psi[p, pl.ds(sub * share, share), :, pl.ds(at, 1)]
            else:
                left = psi[p, pl.ds(sub * share, share), pl.ds(at, 1)]
            left = left.reshape(share * 2 * block_rows, points)
            for level in range(2):
                cols = pl.ds(level * middle + kind * part, part)
                value = jnp.dot(left, flat[p, :, cols], preferred_element_type=f32)
                total = value if total is None else total + value
        return total.reshape(share, 2, block_rows, part)

    mates = [mate_x, mate_y]
    with jax.named_scope("pfin"):
        for kind in range(2):
            for p in range(2):
                got(take.at[kind, p], take_recv.at[kind, p])
                total = back[p, half, :, span(kind)] + take[kind, p].astype(f32)
                high = total.astype(bf16)
                flat[p, :, span(kind)] = high
                low = (total - high.astype(f32)).astype(bf16)
                flat[p, :, pl.ds(middle + kind * part, part)] = low
            for sub in range(SUBS):
                away = [aside, across][kind]
                first_send[kind, sub] = product(kind, away, sub).astype(bf16)
                send(
                    first_send.at[kind, sub],
                    first_got.at[kind, sub],
                    first_recv.at[kind, sub],
                    mates[kind],
                    half,
                    first_send.at[0, 0],
                )
        for sub in range(SUBS):
            for kind in range(2):
                keep[kind, sub] = product(kind, [x, y][kind], sub)

    with jax.named_scope("psecond"):
        for sub in range(SUBS):
            for kind in range(2):
                got(first_got.at[kind, sub], first_recv.at[kind, sub])
                away, home = [(across, y), (aside, x)][kind]

                def summed(at, kind=kind, sub=sub):
                    mine = keep[kind, sub, :, pl.ds(at, 1)]
                    theirs = first_got[kind, sub, :, pl.ds(at, 1)].astype(f32)
                    return (mine + theirs).reshape(share, block_rows, part)

                second_send[kind, sub] = summed(away).astype(bf16)
                send(
                    second_send.at[kind, sub],
                    second_got.at[kind, sub],
                    second_recv.at[kind, sub],
                    mates[1 - kind],
                    half,
                    second_send.at[0, 0],
                )
                keep[kind, sub, :, pl.ds(home, 1)] = summed(home).reshape(
                    share, 1, block_rows, part
                )

    with jax.named_scope("pthird"):
        for sub in range(SUBS):
            for kind in range(2):
                got(second_got.at[kind, sub], second_recv.at[kind, sub])
                home = [y, x][kind]
                mine = keep[kind, sub, :, pl.ds(home, 1)].reshape(share, block_rows, part)
                value = mine + second_got[kind, sub].astype(f32)
                keep[kind, sub, :, pl.ds(home, 1)] = value.reshape(share, 1, block_rows, part)
                third[kind, sub] = value.astype(bf16)
                for i in range(share):
                    zz = sub * share + i
                    for v in range(2):
                        send(
                            third.at[kind, sub, i, pl.ds(v * rows, rows)],
                            parts.at[z, half, kind],
                            parts_recv.at[z, half, kind],
                            tile_of(zz, y, x),
                            v,
                            parts.at[0, 0, 0],
                            (z != zz) | (half != v),
                        )

    with jax.named_scope("psum"):
        for flip in range(2):
            vec = lax.rem(half + flip, 2)
            for kind in range(2):
                value = None
                if flip == 0:
                    home = [y, x][kind]
                    value = keep[
                        kind, z // share, lax.rem(z, share), home, pl.ds(half * rows, rows)
                    ]
                for d in range(layers):
                    if flip == 0 and d == 0:
                        continue
                    zz = lax.rem(z + d, layers)
                    got(parts.at[zz, vec, kind], parts_recv.at[zz, vec, kind])
                    more = parts[zz, vec, kind].astype(f32)
                    value = more if value is None else value + more
                start = pl.multiple_of(vec * middle + kind * part, 128)
                out_ref[:, pl.ds(start, part)] = value

    assert len(pending) <= sends.shape[0]
    for i, (like, *conds) in enumerate(pending):
        wait = remote(like, like, sends.at[i], parts_recv.at[0, 0, 0], me, other).wait_send
        conds = [cond for cond in conds if cond is not None]
        if conds:
            pl.when(functools.reduce(jnp.logical_and, conds))(wait)
        else:
            wait()


def sends_of(layers):
    events = layers - 1
    slots = layers * 2
    count = 1 + 4 + 4 + 1 + 3 * CUTS + slots
    count += events * 8 + layers * 2 + 1
    count += 3 * CUTS * sum(events - e for e in range(events))
    return count + 4 + 2 * SUBS * 2 + 2 * layers * 2


def fused(tiles, trial, psi_v, psi_c, screened):
    rows, conduct = trial.shape[1:]
    valence, points = psi_v.shape
    width = psi_c.shape[2]
    middle = conduct // 2
    part = middle // 2
    layers = tiles // 4
    slots = layers * 2
    share = layers // SUBS
    bf16, f32 = jnp.bfloat16, jnp.float32
    far = pl.BlockSpec(memory_space=pl.ANY)
    dma = pltpu.SemaphoreType.DMA
    vmem = pltpu.VMEM
    out = pl.pallas_call(
        functools.partial(body, layers),
        out_shape=jax.ShapeDtypeStruct((rows, conduct), f32),
        in_specs=[far] * 4,
        out_specs=pl.BlockSpec(memory_space=vmem),
        scratch_shapes=[
            vmem((valence, conduct), bf16),
            vmem((2, layers, 2, 2, 2 * rows, points), bf16),
            vmem((2, points, valence), bf16),
            vmem((slots, points, width), f32),
            vmem((slots, points, width), f32),
            vmem((slots, points, width), bf16),
            vmem((slots, points, width), bf16),
            vmem((slots, conduct, width), bf16),
            vmem((2, points, conduct), bf16),
            vmem((2, 2, points, middle), f32),
            vmem((2, 2, points, part), bf16),
            vmem((2, 2, points, part), bf16),
            vmem((2, SUBS, share, 2, 2 * rows, part), bf16),
            vmem((2, SUBS, share, 2, 2 * rows, part), bf16),
            vmem((2, SUBS, share, 2, 2 * rows, part), f32),
            vmem((2, SUBS, share, 2 * rows, part), bf16),
            vmem((2, SUBS, share, 2 * rows, part), bf16),
            vmem((2, SUBS, share, 2 * rows, part), bf16),
            vmem((layers, 2, 2, rows, part), bf16),
            dma((3 + 2 * slots,)),
            dma((sends_of(layers),)),
            dma((tiles,)),
            dma((tiles,)),
            dma((2,)),
            dma((slots,)),
            dma((slots, CUTS)),
            dma((2, 2)),
            dma((2, SUBS)),
            dma((2, SUBS)),
            dma((layers, 2, 2)),
        ],
        compiler_params=pltpu.CompilerParams(
            collective_id=0, has_side_effects=True, vmem_limit_bytes=58 * 1024 * 1024
        ),
    )(
        trial[0],
        psi_v.reshape(layers, 2, 2, 2 * rows, points),
        psi_c[:, 0, :],
        screened,
    )
    return out[None]


def solution(mesh):
    tiles = mesh.shape["tile"]

    def shards(trial, psi_v, psi_c, screened):
        fits = (
            trial.shape[0] == 1
            and mesh.shape["vec"] == 2
            and tiles % (4 * SUBS) == 0
            and psi_v.shape[1] % 128 == 0
            and psi_c.shape[2] % 128 == 0
            and trial.shape[1] % 16 == 0
            and trial.shape[2] % 512 == 0
        )
        if fits:
            return fused(tiles, trial, psi_v, psi_c, screened)
        return plain(trial, psi_v, psi_c, screened)

    in_specs = (
        P(None, ("tile", "vec"), None),
        P(None, "tile"),
        P(None, "vec", "tile"),
        P("tile", "vec"),
    )
    out_specs = P(None, ("tile", "vec"), None)
    return jax.shard_map(shards, mesh=mesh, in_specs=in_specs, out_specs=out_specs, check_vma=False)
```

time: 118 us -> 98.7 us (0.84)
  the two profiles are of different devices: /device:TPU:15 before, /device:TPU:0 now
where the time goes in v1:
time: 98.7 us; the launch traced here: 98.2 us
  Pallas kernels  96.6 us (98%)
  local copies, waits for them, and re-layouts  1.57 us (2%)
    pallas_call x1, Pallas kernels, fused(): pl.pallas_call(functools.partial(body, layers), out_shape=jax.ShapeDtypeS...  96.6 us

profile of v1, /device:TPU:0, one launch (start us, length us, event | category | flops | bytes accessed | tf_op | source)
XLA Modules:
  0.0 98.2 jit_solution(8105422046535715935)
XLA Ops:
  0.0 96.6 %shard_map.46 = f32[32,1024]{1,0:T(8,128)} custom-call(bf16[32,1024]{1,0:T(8,128)(2,1)} %bitcast.7, bf16[4,2,2,64,512]{4,3,2,1,0:T(8,128)(2,1)} %bitcast.4, bf16[1024,256]{1,0:T(8,128)(2,1)} %bitcast.6, f32[512,4096]{1,0:T(8,128)} %screened_hbm.1), custom_call_target="tpu_custom_call" | custom-call | tf_op jit(solution)/shard_map/pallas_call | solution.py:532
  96.6 1.6 %copy.6 = f32[1,32,1024]{2,1,0:T(8,128)} copy(f32[1,32,1024]{2,1,0:T(8,128)} %bitcast.5) | data formatting | bytes 262144

commit v2 on v1

--- a/solution.py
+++ b/solution.py
@@ -85,6 +85,7 @@
     first_send,
     first_got,
     keep,
+    leave,
     second_send,
     second_got,
     third,
@@ -226,14 +227,29 @@
         send(src, dst, recv, mate_y, half, some_rows)
         hand(src, tile)
 
-    def own_piece(s):
-        src = piece(psi_c_hbm, s)
-        slot = slot_of(z, y)
+    last = CUTS - 1
+    home_slot, mate_slot = slot_of(z, y), slot_of(z, across)
+
+    def along(src, slot, s, to_up, to_down):
         dst = piece(panel.at[slot], s)
         recv = block_recv.at[slot, s]
-        send(src, dst, recv, tile_of(up, y, x), half, some_piece, has_up)
-        send(src, dst, recv, tile_of(down, y, x), half, some_piece, has_down)
-        send(src, dst, recv, mate_y, half, some_piece)
+        send(src, dst, recv, tile_of(up, y, x), half, some_piece, to_up)
+        send(src, dst, recv, tile_of(down, y, x), half, some_piece, to_down)
+
+    def cross(src, slot, s):
+        dst = piece(panel.at[slot], s)
+        send(src, dst, block_recv.at[slot, s], mate_y, half, some_piece)
+
+    def own_piece_z(s):
+        along(piece(psi_c_hbm, s), home_slot, s, has_up, has_down)
+
+    def own_piece_y(s):
+        cross(piece(psi_c_hbm, s), home_slot, s)
+
+    def came(slot, s):
+        ref = piece(panel.at[slot], s)
+        got(ref, block_recv.at[slot, s])
+        return ref
 
     pair_layers = layers // 2
 
@@ -243,7 +259,6 @@
     with jax.named_scope("ptrial"):
         send(trial_hbm, lines(me, half), trial_recv.at[me], mate_x, half, some_rows)
         spread(trial_hbm, me, has_up, has_down)
-        own_piece(0)
         send(
             psi_half(psi_v_hbm, half),
             psi_half(psi.at[1], half),
@@ -274,10 +289,14 @@
                 ref = lines(tile, half)
                 got(ref, trial_recv.at[tile])
                 spread(ref, tile, on_up[e], on_down[e])
-            if e + 1 < CUTS:
-                own_piece(e + 1)
-        for s in range(events + 1, CUTS):
-            own_piece(s)
+            if e == events - 2:
+                own_piece_y(last)
+                own_piece_z(0)
+        for s in range(CUTS):
+            if s < last:
+                own_piece_y(s)
+            if s > 0:
+                own_piece_z(s)
 
         back[...] = jnp.zeros_like(back)
         load_psi.wait()
@@ -295,6 +314,7 @@
         got(ref, psi_recv.at[0])
         send(ref, ref, psi_recv.at[1], me, other, psi_half(psi.at[1], 0))
         load_rows.wait()
+        along(came(mate_slot, last), mate_slot, last, has_up, has_down)
         for tile in range(layers * 4):
             got(lines(tile, other), hand_recv.at[tile])
 
@@ -319,12 +339,12 @@
     def arrive(e):
         slot = slot_of(source[e], y)
         for s in range(CUTS):
-            ref = piece(panel.at[slot], s)
-            recv = block_recv.at[slot, s]
-            got(ref, recv)
-            send(ref, ref, recv, mate_y, half, some_piece, None)
-            send(ref, ref, recv, tile_of(up, y, x), half, some_piece, on_up[e])
-            send(ref, ref, recv, tile_of(down, y, x), half, some_piece, on_down[e])
+            ref = came(slot, s)
+            along(ref, slot, s, on_up[e], on_down[e])
+            if s < last:
+                cross(ref, slot, s)
+        slot = slot_of(source[e], across)
+        along(came(slot, last), slot, last, on_up[e], on_down[e])
 
     def arrive_if(e, k):
         start = len(pending)
@@ -342,9 +362,8 @@
             for late in range(e, events):
                 arrive_if(late, e + 1)
         if kind == "y":
-            slot = turns[i]
-            for s in range(CUTS):
-                got(piece(panel.at[slot], s), block_recv.at[slot, s])
+            for s in range(last):
+                came(turns[i], s)
         load_own[i].wait()
 
     def step(p, share, slot):
@@ -358,7 +377,7 @@
 
     def use(k, carry):
         slot = turns[0]
-        for i in range(slots):
+        for i in range(final):
             slot = jnp.where(k == i, turns[i], slot)
 
             @pl.when(k == i)
@@ -370,55 +389,87 @@
         step(1, screened_in[k], slot)
         return carry
 
+    final = slots - 1
     with jax.named_scope("puse"):
-        lax.fori_loop(0, slots, use, 0)
+        lax.fori_loop(0, final, use, 0)
+        receive(final)
+        step(0, screened_own[final], turns[final])
 
     def span(kind):
         return pl.ds(kind * part, part)
 
-    with jax.named_scope("pswap"):
+    def swap(p):
         for kind in range(2):
-            for p in range(2):
-                give[kind, p] = back[p, other, :, span(kind)].astype(bf16)
-                send(
-                    give.at[kind, p],
-                    take.at[kind, p],
-                    take_recv.at[kind, p],
-                    me,
-                    other,
-                    give.at[0, 0],
-                )
+            give[kind, p] = back[p, other, :, span(kind)].astype(bf16)
+            send(
+                give.at[kind, p],
+                take.at[kind, p],
+                take_recv.at[kind, p],
+                me,
+                other,
+                give.at[0, 0],
+            )
+
+    def split(kind, p):
+        got(take.at[kind, p], take_recv.at[kind, p])
+        total = back[p, half, :, span(kind)] + take[kind, p].astype(f32)
+        high = total.astype(bf16)
+        flat[p, :, span(kind)] = high
+        low = (total - high.astype(f32)).astype(bf16)
+        flat[p, :, pl.ds(middle + kind * part, part)] = low
 
     share = layers // SUBS
     block_rows = 2 * rows
 
-    def product(kind, at, sub):
+    def product(p, kind, at, sub):
+        if kind == 0:
+            left = psi[p, pl.ds(sub * share, share), :, pl.ds(at, 1)]
+        else:
+            left = psi[p, pl.ds(sub * share, share), pl.ds(at, 1)]
+        left = left.reshape(share * 2 * block_rows, points)
         total = None
-        for p in range(2):
-            if kind == 0:
-                left = psi[p, pl.ds(sub * share, share), :, pl.ds(at, 1)]
+        for level in range(2):
+            cols = pl.ds(level * middle + kind * part, part)
+            value = jnp.dot(left, flat[p, :, cols], preferred_element_type=f32)
+            total = value if total is None else total + value
+        return total.reshape(share, 2, block_rows, part)
+
+    settled = [0]
+
+    def settle():
+        for i in range(settled[0], len(pending)):
+            like, *conds = pending[i]
+            wait = remote(like, like, sends.at[i], parts_recv.at[0, 0, 0], me, other).wait_send
+            conds = [cond for cond in conds if cond is not None]
+            if conds:
+                pl.when(functools.reduce(jnp.logical_and, conds))(wait)
             else:
-                left = psi[p, pl.ds(sub * share, share), pl.ds(at, 1)]
-            left = left.reshape(share * 2 * block_rows, points)
-            for level in range(2):
-                cols = pl.ds(level * middle + kind * part, part)
-                value = jnp.dot(left, flat[p, :, cols], preferred_element_type=f32)
-                total = value if total is None else total + value
-        return total.reshape(share, 2, block_rows, part)
+                wait()
+        settled[0] = len(pending)
 
     mates = [mate_x, mate_y]
+    homes, aways = [x, y], [aside, across]
+    with jax.named_scope("pearly"):
+        swap(0)
+        for kind in range(2):
+            split(kind, 0)
+        for sub in range(SUBS):
+            for kind in range(2):
+                keep[kind, sub] = product(0, kind, homes[kind], sub)
+                leave[kind, sub] = product(0, kind, aways[kind], sub)
+
+    with jax.named_scope("plast"):
+        got(screened_in.at[final], screened_recv.at[final])
+        step(1, screened_in[final], turns[final])
+
     with jax.named_scope("pfin"):
-        for kind in range(2):
-            for p in range(2):
-                got(take.at[kind, p], take_recv.at[kind, p])
-                total = back[p, half, :, span(kind)] + take[kind, p].astype(f32)
-                high = total.astype(bf16)
-                flat[p, :, span(kind)] = high
-                low = (total - high.astype(f32)).astype(bf16)
-                flat[p, :, pl.ds(middle + kind * part, part)] = low
-            for sub in range(SUBS):
-                away = [aside, across][kind]
-                first_send[kind, sub] = product(kind, away, sub).astype(bf16)
+        swap(1)
+        for sub in range(SUBS):
+            for kind in range(2):
+                if sub == 0:
+                    split(kind, 1)
+                value = leave[kind, sub] + product(1, kind, aways[kind], sub)
+                first_send[kind, sub] = value.astype(bf16)
                 send(
                     first_send.at[kind, sub],
                     first_got.at[kind, sub],
@@ -429,7 +480,10 @@
                 )
         for sub in range(SUBS):
             for kind in range(2):
-                keep[kind, sub] = product(kind, [x, y][kind], sub)
+                keep[kind, sub] += product(1, kind, homes[kind], sub)
+
+    with jax.named_scope("psettle"):
+        settle()
 
     with jax.named_scope("psecond"):
         for sub in range(SUBS):
@@ -498,13 +552,7 @@
                 out_ref[:, pl.ds(start, part)] = value
 
     assert len(pending) <= sends.shape[0]
-    for i, (like, *conds) in enumerate(pending):
-        wait = remote(like, like, sends.at[i], parts_recv.at[0, 0, 0], me, other).wait_send
-        conds = [cond for cond in conds if cond is not None]
-        if conds:
-            pl.when(functools.reduce(jnp.logical_and, conds))(wait)
-        else:
-            wait()
+    settle()
 
 
 def sends_of(layers):
@@ -512,7 +560,7 @@
     slots = layers * 2
     count = 1 + 4 + 4 + 1 + 3 * CUTS + slots
     count += events * 8 + layers * 2 + 1
-    count += 3 * CUTS * sum(events - e for e in range(events))
+    count += 2 + (3 * CUTS + 2) * sum(events - e for e in range(events))
     return count + 4 + 2 * SUBS * 2 + 2 * layers * 2
 
 
@@ -550,6 +598,7 @@
             vmem((2, SUBS, share, 2, 2 * rows, part), bf16),
             vmem((2, SUBS, share, 2, 2 * rows, part), bf16),
             vmem((2, SUBS, share, 2, 2 * rows, part), f32),
+            vmem((2, SUBS, share, 2, 2 * rows, part), f32),
             vmem((2, SUBS, share, 2 * rows, part), bf16),
             vmem((2, SUBS, share, 2 * rows, part), bf16),
             vmem((2, SUBS, share, 2 * rows, part), bf16),

time: 98.7 us -> 95.1 us (0.964)
  Pallas kernels: 96.6 us -> 93.4 us
    pallas_call x1, Pallas kernels: 96.6 us -> 93.4 us  [fused(): pl.pallas_call(functools.partial(body, layers), out_shape=jax.ShapeDtypeS...]
where the time goes in v2:
time: 95.1 us; the launch traced here: 95 us
  Pallas kernels  93.4 us (98%)
  local copies, waits for them, and re-layouts  1.57 us (2%)
    pallas_call x1, Pallas kernels, fused(): pl.pallas_call(functools.partial(body, layers), out_shape=jax.ShapeDtypeS...  93.4 us

profile of v2, /device:TPU:0, one launch (start us, length us, event | category | flops | bytes accessed | tf_op | source)
XLA Modules:
  0.0 95.0 jit_solution(15883532973439086081)
XLA Ops:
  0.0 93.4 %shard_map.46 = f32[32,1024]{1,0:T(8,128)} custom-call(bf16[32,1024]{1,0:T(8,128)(2,1)} %bitcast.7, bf16[4,2,2,64,512]{4,3,2,1,0:T(8,128)(2,1)} %bitcast.4, bf16[1024,256]{1,0:T(8,128)(2,1)} %bitcast.6, f32[512,4096]{1,0:T(8,128)} %screened_hbm.1), custom_call_target="tpu_custom_call" | custom-call | tf_op jit(solution)/shard_map/pallas_call | solution.py:580
  93.4 1.6 %copy.6 = f32[1,32,1024]{2,1,0:T(8,128)} copy(f32[1,32,1024]{2,1,0:T(8,128)} %bitcast.5) | data formatting | bytes 262144

commit v3 on v2

--- a/solution.py
+++ b/solution.py
@@ -161,17 +161,9 @@
         local.append(copy)
         return copy
 
+    load_rows = load(trial_hbm, lines(me, half))
     load_psi = load(psi_v_hbm, psi.at[0])
-    load_rows = load(trial_hbm, lines(me, half))
-    load_out = [
-        load(screened_hbm.at[:, columns(turn * 2 + aside)], stage.at[i])
-        for i, turn in enumerate(turns)
-    ]
     load_block = load(psi_c_hbm, panel.at[slot_of(z, y)])
-    load_own = [
-        load(screened_hbm.at[:, columns(turn * 2 + x)], screened_own.at[i])
-        for i, turn in enumerate(turns)
-    ]
 
     def remote(src, dst, send, recv, tile, vec):
         return pltpu.make_async_remote_copy(
@@ -219,13 +211,14 @@
     def hand(src, tile):
         send(src, lines(tile, half), hand_recv.at[tile], me, other, some_rows)
 
-    def spread(src, tile, to_up, to_down):
-        dst = lines(tile, half)
+    def spread(tile, column):
+        ref = lines(tile, half)
         recv = trial_recv.at[tile]
-        send(src, dst, recv, tile_of(up, y, x), half, some_rows, to_up)
-        send(src, dst, recv, tile_of(down, y, x), half, some_rows, to_down)
-        send(src, dst, recv, mate_y, half, some_rows)
-        hand(src, tile)
+        if column:
+            for e in range(events):
+                send(ref, ref, recv, tile_of(source[e], y, x), half, some_rows)
+        send(ref, ref, recv, mate_y, half, some_rows)
+        hand(ref, tile)
 
     last = CUTS - 1
     home_slot, mate_slot = slot_of(z, y), slot_of(z, across)
@@ -241,10 +234,10 @@
         send(src, dst, block_recv.at[slot, s], mate_y, half, some_piece)
 
     def own_piece_z(s):
-        along(piece(psi_c_hbm, s), home_slot, s, has_up, has_down)
+        along(piece(panel.at[home_slot], s), home_slot, s, has_up, has_down)
 
     def own_piece_y(s):
-        cross(piece(psi_c_hbm, s), home_slot, s)
+        cross(piece(panel.at[home_slot], s), home_slot, s)
 
     def came(slot, s):
         ref = piece(panel.at[slot], s)
@@ -257,10 +250,21 @@
         return ref.at[pl.ds(which * pair_layers, pair_layers)]
 
     with jax.named_scope("ptrial"):
-        send(trial_hbm, lines(me, half), trial_recv.at[me], mate_x, half, some_rows)
-        spread(trial_hbm, me, has_up, has_down)
+        ref = lines(me, half)
+        load_rows.wait()
+        send(ref, ref, trial_recv.at[me], mate_x, half, some_rows)
+        spread(me, True)
+        load_out = [
+            load(screened_hbm.at[:, columns(turn * 2 + aside)], stage.at[i])
+            for i, turn in enumerate(turns)
+        ]
+        load_own = [
+            load(screened_hbm.at[:, columns(turn * 2 + x)], screened_own.at[i])
+            for i, turn in enumerate(turns)
+        ]
+        load_psi.wait()
         send(
-            psi_half(psi_v_hbm, half),
+            psi_half(psi.at[0], half),
             psi_half(psi.at[1], half),
             psi_recv.at[0],
             mate_x,
@@ -268,7 +272,11 @@
             psi_half(psi.at[1], 0),
         )
         got(lines(mate_x, half), trial_recv.at[mate_x])
-        spread(lines(mate_x, half), mate_x, has_up, has_down)
+        spread(mate_x, True)
+        load_block.wait()
+        own_piece_y(last)
+        for s in range(CUTS):
+            own_piece_z(s)
 
         for i in range(slots):
             load_out[i].wait()
@@ -286,20 +294,12 @@
         for e in range(events):
             for xx in range(2):
                 tile = tile_of(source[e], y, xx)
-                ref = lines(tile, half)
-                got(ref, trial_recv.at[tile])
-                spread(ref, tile, on_up[e], on_down[e])
-            if e == events - 2:
-                own_piece_y(last)
-                own_piece_z(0)
-        for s in range(CUTS):
-            if s < last:
-                own_piece_y(s)
-            if s > 0:
-                own_piece_z(s)
+                got(lines(tile, half), trial_recv.at[tile])
+                spread(tile, False)
+        for s in range(last):
+            own_piece_y(s)
 
         back[...] = jnp.zeros_like(back)
-        load_psi.wait()
         valence = layers * 4 * 2 * rows
         psi_t[0] = psi[0].reshape(valence, points).T
 
@@ -313,7 +313,6 @@
         ref = psi_half(psi.at[1], half)
         got(ref, psi_recv.at[0])
         send(ref, ref, psi_recv.at[1], me, other, psi_half(psi.at[1], 0))
-        load_rows.wait()
         along(came(mate_slot, last), mate_slot, last, has_up, has_down)
         for tile in range(layers * 4):
             got(lines(tile, other), hand_recv.at[tile])
@@ -372,8 +371,6 @@
         weighted = (share.astype(f32) * pair).astype(bf16)
         for h in range(2):
             back[p, h] += back_product(weighted, block[pl.ds(h * middle, middle), :])
-
-    load_block.wait()
 
     def use(k, carry):
         slot = turns[0]
@@ -558,8 +555,8 @@
 def sends_of(layers):
     events = layers - 1
     slots = layers * 2
-    count = 1 + 4 + 4 + 1 + 3 * CUTS + slots
-    count += events * 8 + layers * 2 + 1
+    count = 1 + 2 * (events + 2) + 1 + 3 * CUTS + slots
+    count += events * 4 + layers * 2 + 1
     count += 2 + (3 * CUTS + 2) * sum(events - e for e in range(events))
     return count + 4 + 2 * SUBS * 2 + 2 * layers * 2
 

time: 95.1 us -> 97.6 us (1.026)
  Pallas kernels: 93.4 us -> 95.9 us
    pallas_call x1, Pallas kernels: 93.4 us -> 95.9 us  [fused(): pl.pallas_call(functools.partial(body, layers), out_shape=jax.ShapeDtypeS...]
where the time goes in v3:
time: 97.6 us; the launch traced here: 97.4 us
  Pallas kernels  95.9 us (98%)
  local copies, waits for them, and re-layouts  1.57 us (2%)
    pallas_call x1, Pallas kernels, fused(): pl.pallas_call(functools.partial(body, layers), out_shape=jax.ShapeDtypeS...  95.9 us

profile of v3, /device:TPU:0, one launch (start us, length us, event | category | flops | bytes accessed | tf_op | source)
XLA Modules:
  0.0 97.4 jit_solution(16442807463530873118)
XLA Ops:
  0.0 95.9 %shard_map.46 = f32[32,1024]{1,0:T(8,128)} custom-call(bf16[32,1024]{1,0:T(8,128)(2,1)} %bitcast.7, bf16[4,2,2,64,512]{4,3,2,1,0:T(8,128)(2,1)} %bitcast.4, bf16[1024,256]{1,0:T(8,128)(2,1)} %bitcast.6, f32[512,4096]{1,0:T(8,128)} %screened_hbm.1), custom_call_target="tpu_custom_call" | custom-call | tf_op jit(solution)/shard_map/pallas_call | solution.py:577
  95.9 1.6 %copy.6 = f32[1,32,1024]{2,1,0:T(8,128)} copy(f32[1,32,1024]{2,1,0:T(8,128)} %bitcast.5) | data formatting | bytes 262144

commit v4 on v3

--- a/solution.py
+++ b/solution.py
@@ -69,7 +69,8 @@
     psi_v_hbm,
     psi_c_hbm,
     screened_hbm,
-    out_ref,
+    out_hbm,
+    result,
     whole,
     psi,
     psi_t,
@@ -249,6 +250,26 @@
     def psi_half(ref, which):
         return ref.at[pl.ds(which * pair_layers, pair_layers)]
 
+    def arrive(e):
+        slot = slot_of(source[e], y)
+        for s in range(CUTS):
+            ref = came(slot, s)
+            along(ref, slot, s, on_up[e], on_down[e])
+            if s < last:
+                cross(ref, slot, s)
+        slot = slot_of(source[e], across)
+        along(came(slot, last), slot, last, on_up[e], on_down[e])
+
+    def arrive_if(e, k):
+        start = len(pending)
+
+        @pl.when(at_distance[e][k])
+        def _():
+            arrive(e)
+
+        for i in range(start, len(pending)):
+            pending[i] += (at_distance[e][k],)
+
     with jax.named_scope("ptrial"):
         ref = lines(me, half)
         load_rows.wait()
@@ -275,8 +296,6 @@
         spread(mate_x, True)
         load_block.wait()
         own_piece_y(last)
-        for s in range(CUTS):
-            own_piece_z(s)
 
         for i in range(slots):
             load_out[i].wait()
@@ -296,6 +315,9 @@
                 tile = tile_of(source[e], y, xx)
                 got(lines(tile, half), trial_recv.at[tile])
                 spread(tile, False)
+            if e == max(events - 2, 0):
+                for s in range(CUTS):
+                    own_piece_z(s)
         for s in range(last):
             own_piece_y(s)
 
@@ -314,6 +336,8 @@
         got(ref, psi_recv.at[0])
         send(ref, ref, psi_recv.at[1], me, other, psi_half(psi.at[1], 0))
         along(came(mate_slot, last), mate_slot, last, has_up, has_down)
+        for e in range(events):
+            arrive_if(e, 1)
         for tile in range(layers * 4):
             got(lines(tile, other), hand_recv.at[tile])
 
@@ -335,29 +359,9 @@
         psi_t[1] = psi[1].reshape(valence, points).T
         project(1)
 
-    def arrive(e):
-        slot = slot_of(source[e], y)
-        for s in range(CUTS):
-            ref = came(slot, s)
-            along(ref, slot, s, on_up[e], on_down[e])
-            if s < last:
-                cross(ref, slot, s)
-        slot = slot_of(source[e], across)
-        along(came(slot, last), slot, last, on_up[e], on_down[e])
-
-    def arrive_if(e, k):
-        start = len(pending)
-
-        @pl.when(at_distance[e][k])
-        def _():
-            arrive(e)
-
-        for i in range(start, len(pending)):
-            pending[i] += (at_distance[e][k],)
-
     def receive(i):
         kind, e = order[i]
-        if kind == "z":
+        if kind == "z" and e > 0:
             for late in range(e, events):
                 arrive_if(late, e + 1)
         if kind == "y":
@@ -433,8 +437,8 @@
 
     settled = [0]
 
-    def settle():
-        for i in range(settled[0], len(pending)):
+    def settle(upto):
+        for i in range(settled[0], upto):
             like, *conds = pending[i]
             wait = remote(like, like, sends.at[i], parts_recv.at[0, 0, 0], me, other).wait_send
             conds = [cond for cond in conds if cond is not None]
@@ -442,7 +446,7 @@
                 pl.when(functools.reduce(jnp.logical_and, conds))(wait)
             else:
                 wait()
-        settled[0] = len(pending)
+        settled[0] = upto
 
     mates = [mate_x, mate_y]
     homes, aways = [x, y], [aside, across]
@@ -459,6 +463,7 @@
         got(screened_in.at[final], screened_recv.at[final])
         step(1, screened_in[final], turns[final])
 
+    earlier = len(pending)
     with jax.named_scope("pfin"):
         swap(1)
         for sub in range(SUBS):
@@ -480,7 +485,7 @@
                 keep[kind, sub] += product(1, kind, homes[kind], sub)
 
     with jax.named_scope("psettle"):
-        settle()
+        settle(earlier)
 
     with jax.named_scope("psecond"):
         for sub in range(SUBS):
@@ -545,11 +550,14 @@
                     got(parts.at[zz, vec, kind], parts_recv.at[zz, vec, kind])
                     more = parts[zz, vec, kind].astype(f32)
                     value = more if value is None else value + more
-                start = pl.multiple_of(vec * middle + kind * part, 128)
-                out_ref[:, pl.ds(start, part)] = value
+                block = pl.ds(pl.multiple_of(vec * middle + kind * part, 128), part)
+                result[:, block] = value
+                load(result.at[:, block], out_hbm.at[:, block])
 
     assert len(pending) <= sends.shape[0]
-    settle()
+    settle(len(pending))
+    for copy in local[-4:]:
+        copy.wait()
 
 
 def sends_of(layers):
@@ -578,8 +586,9 @@
         functools.partial(body, layers),
         out_shape=jax.ShapeDtypeStruct((rows, conduct), f32),
         in_specs=[far] * 4,
-        out_specs=pl.BlockSpec(memory_space=vmem),
+        out_specs=far,
         scratch_shapes=[
+            vmem((rows, conduct), f32),
             vmem((valence, conduct), bf16),
             vmem((2, layers, 2, 2, 2 * rows, points), bf16),
             vmem((2, points, valence), bf16),
@@ -600,7 +609,7 @@
             vmem((2, SUBS, share, 2 * rows, part), bf16),
             vmem((2, SUBS, share, 2 * rows, part), bf16),
             vmem((layers, 2, 2, rows, part), bf16),
-            dma((3 + 2 * slots,)),
+            dma((3 + 2 * slots + 4,)),
             dma((sends_of(layers),)),
             dma((tiles,)),
             dma((tiles,)),

time: 97.6 us -> 92.7 us (0.950)
  Pallas kernels: 95.9 us -> 91 us
    pallas_call x1, Pallas kernels: 95.9 us -> 91 us  [fused(): pl.pallas_call(functools.partial(body, layers), out_shape=jax.ShapeDtypeS...]
where the time goes in v4:
time: 92.7 us; the launch traced here: 92.6 us
  Pallas kernels  91 us (98%)
  local copies, waits for them, and re-layouts  1.57 us (2%)
    pallas_call x1, Pallas kernels, fused(): pl.pallas_call(functools.partial(body, layers), out_shape=jax.ShapeDtypeS...  91 us

profile of v4, /device:TPU:0, one launch (start us, length us, event | category | flops | bytes accessed | tf_op | source)
XLA Modules:
  0.0 92.6 jit_solution(9587073796786139550)
XLA Ops:
  0.0 91.0 %shard_map.46 = f32[32,1024]{1,0:T(8,128)} custom-call(bf16[32,1024]{1,0:T(8,128)(2,1)} %bitcast.7, bf16[4,2,2,64,512]{4,3,2,1,0:T(8,128)(2,1)} %bitcast.4, bf16[1024,256]{1,0:T(8,128)(2,1)} %bitcast.6, f32[512,4096]{1,0:T(8,128)} %screened_hbm.1), custom_call_target="tpu_custom_call" | custom-call | tf_op jit(solution)/shard_map/pallas_call | solution.py:585
  91.0 1.6 %copy.6 = f32[1,32,1024]{2,1,0:T(8,128)} copy(f32[1,32,1024]{2,1,0:T(8,128)} %bitcast.5) | data formatting | bytes 262144

commit v5 on v4

--- a/solution.py
+++ b/solution.py
@@ -9,6 +9,7 @@
 
 CUTS = 4
 SUBS = 2
+ROWS, ACROSS, LAYERS, SHARE, POINTS, GIVE, FIRST, SECOND, THIRD = range(9)
 
 
 def back_product(weighted_flat, panel):
@@ -69,7 +70,6 @@
     psi_v_hbm,
     psi_c_hbm,
     screened_hbm,
-    out_hbm,
     result,
     whole,
     psi,
@@ -130,9 +130,9 @@
 
     slots = layers * 2
     order = [("own", 0)]
-    for e in range(events):
+    for e in range(events - 1):
         order += [("z", e), ("y", e - 1)]
-    order += [("y", events - 1)]
+    order += [("y", events - 2), ("z", events - 1), ("y", events - 1)]
 
     def slot_at(kind, e):
         zz = source[e] if e >= 0 and kind != "own" else z
@@ -154,17 +154,19 @@
     def columns(tile):
         return pl.ds(pl.multiple_of(tile * width, 128), width)
 
-    local = []
-
-    def load(src, dst):
-        copy = pltpu.make_async_copy(src, dst, local_sem.at[len(local)])
+    def load(src, dst, sem):
+        copy = pltpu.make_async_copy(src, dst, local_sem.at[sem])
         copy.start()
-        local.append(copy)
         return copy
 
-    load_rows = load(trial_hbm, lines(me, half))
-    load_psi = load(psi_v_hbm, psi.at[0])
-    load_block = load(psi_c_hbm, panel.at[slot_of(z, y)])
+    home_slot, mate_slot = slot_of(z, y), slot_of(z, across)
+
+    def block_of(slot):
+        return panel.at[pl.ds(pl.multiple_of(slot * conduct, conduct), conduct), :]
+
+    load_rows = load(trial_hbm, lines(me, half), 0)
+    load_psi = load(psi_v_hbm, psi.at[0], 1)
+    load_block = load(psi_c_hbm, block_of(home_slot), 2)
 
     def remote(src, dst, send, recv, tile, vec):
         return pltpu.make_async_remote_copy(
@@ -188,127 +190,101 @@
             )
         pl.semaphore_wait(barrier, len(partners))
 
-    pending = []
-
-    def send(src, dst, recv, tile, vec, like, cond=None):
-        i = len(pending)
-        copy = remote(src, dst, sends.at[i], recv, tile, vec)
-        pending.append((like, cond))
+    def send(src, dst, group, recv, tile, vec, cond=None):
+        copy = remote(src, dst, sends.at[group], recv, tile, vec)
         if cond is None:
             copy.start()
         else:
             pl.when(cond)(copy.start)
 
+    def sent(ref, group):
+        remote(ref, ref, sends.at[group], psi_recv.at[0], me, other).wait_send()
+
     def got(ref, recv):
         remote(ref, ref, sends.at[0], recv, me, other).wait_recv()
 
-    some_rows = whole.at[pl.ds(0, rows), :]
-
-    def piece(ref, s):
-        return ref.at[pl.ds(s * height, height), :]
-
-    some_piece = piece(panel.at[0], 0)
-
-    def hand(src, tile):
-        send(src, lines(tile, half), hand_recv.at[tile], me, other, some_rows)
+    def piece(slot, s):
+        start = pl.multiple_of(slot * conduct + s * height, height)
+        return panel.at[pl.ds(start, height), :]
+
+    def hand(tile):
+        ref = lines(tile, half)
+        send(ref, ref, ROWS, hand_recv.at[0], me, other)
 
     def spread(tile, column):
         ref = lines(tile, half)
         recv = trial_recv.at[tile]
         if column:
             for e in range(events):
-                send(ref, ref, recv, tile_of(source[e], y, x), half, some_rows)
-        send(ref, ref, recv, mate_y, half, some_rows)
-        hand(ref, tile)
+                send(ref, ref, ROWS, recv, tile_of(source[e], y, x), half)
+        send(ref, ref, ROWS, recv, mate_y, half)
+        hand(tile)
 
     last = CUTS - 1
-    home_slot, mate_slot = slot_of(z, y), slot_of(z, across)
-
-    def along(src, slot, s, to_up, to_down):
-        dst = piece(panel.at[slot], s)
+
+    def along(slot, s, to_up, to_down):
+        ref = piece(slot, s)
         recv = block_recv.at[slot, s]
-        send(src, dst, recv, tile_of(up, y, x), half, some_piece, to_up)
-        send(src, dst, recv, tile_of(down, y, x), half, some_piece, to_down)
-
-    def cross(src, slot, s):
-        dst = piece(panel.at[slot], s)
-        send(src, dst, block_recv.at[slot, s], mate_y, half, some_piece)
-
-    def own_piece_z(s):
-        along(piece(panel.at[home_slot], s), home_slot, s, has_up, has_down)
-
-    def own_piece_y(s):
-        cross(piece(panel.at[home_slot], s), home_slot, s)
+        send(ref, ref, LAYERS, recv, tile_of(up, y, x), half, to_up)
+        send(ref, ref, LAYERS, recv, tile_of(down, y, x), half, to_down)
+
+    def cross(slot, s):
+        ref = piece(slot, s)
+        send(ref, ref, ACROSS, block_recv.at[slot, s], mate_y, half)
 
     def came(slot, s):
-        ref = piece(panel.at[slot], s)
-        got(ref, block_recv.at[slot, s])
-        return ref
+        got(piece(slot, s), block_recv.at[slot, s])
 
     pair_layers = layers // 2
 
     def psi_half(ref, which):
         return ref.at[pl.ds(which * pair_layers, pair_layers)]
 
-    def arrive(e):
+    def take_piece(e, s):
         slot = slot_of(source[e], y)
-        for s in range(CUTS):
-            ref = came(slot, s)
-            along(ref, slot, s, on_up[e], on_down[e])
-            if s < last:
-                cross(ref, slot, s)
+        came(slot, s)
+        along(slot, s, on_up[e], on_down[e])
+        if s < last:
+            cross(slot, s)
+
+    def take_mate(e):
         slot = slot_of(source[e], across)
-        along(came(slot, last), slot, last, on_up[e], on_down[e])
-
-    def arrive_if(e, k):
-        start = len(pending)
-
-        @pl.when(at_distance[e][k])
-        def _():
-            arrive(e)
-
-        for i in range(start, len(pending)):
-            pending[i] += (at_distance[e][k],)
+        came(slot, last)
+        along(slot, last, on_up[e], on_down[e])
+
+    def at_k(k):
+        return [e for e in range(events) if any(abs(row[e] - r) == k for r, row in enumerate(table))]
+
+    def arrive(k, first, final):
+        for s in range(first, final):
+            for e in at_k(k):
+                pl.when(at_distance[e][k])(functools.partial(take_piece, e, s))
+        if final == CUTS:
+            for e in at_k(k):
+                pl.when(at_distance[e][k])(functools.partial(take_mate, e))
 
     with jax.named_scope("ptrial"):
         ref = lines(me, half)
         load_rows.wait()
-        send(ref, ref, trial_recv.at[me], mate_x, half, some_rows)
+        send(ref, ref, ROWS, trial_recv.at[me], mate_x, half)
         spread(me, True)
-        load_out = [
-            load(screened_hbm.at[:, columns(turn * 2 + aside)], stage.at[i])
-            for i, turn in enumerate(turns)
-        ]
-        load_own = [
-            load(screened_hbm.at[:, columns(turn * 2 + x)], screened_own.at[i])
-            for i, turn in enumerate(turns)
-        ]
+        for i, turn in enumerate(turns):
+            load(screened_hbm.at[:, columns(turn * 2 + aside)], stage.at[i], 3)
+        for i, turn in enumerate(turns):
+            load(screened_hbm.at[:, columns(turn * 2 + x)], screened_own.at[i], 4)
         load_psi.wait()
-        send(
-            psi_half(psi.at[0], half),
-            psi_half(psi.at[1], half),
-            psi_recv.at[0],
-            mate_x,
-            half,
-            psi_half(psi.at[1], 0),
-        )
+        ref = psi_half(psi.at[0], half)
+        send(ref, psi_half(psi.at[1], half), POINTS, psi_recv.at[0], mate_x, half)
         got(lines(mate_x, half), trial_recv.at[mate_x])
         spread(mate_x, True)
         load_block.wait()
-        own_piece_y(last)
-
+        cross(home_slot, last)
+
+        pltpu.make_async_copy(stage, stage, local_sem.at[3]).wait()
         for i in range(slots):
-            load_out[i].wait()
             screened_out[i] = stage[i].astype(bf16)
         for i in range(slots):
-            send(
-                screened_out.at[i],
-                screened_in.at[i],
-                screened_recv.at[i],
-                mate_x,
-                half,
-                screened_out.at[0],
-            )
+            send(screened_out.at[i], screened_in.at[i], SHARE, screened_recv.at[i], mate_x, half)
 
         for e in range(events):
             for xx in range(2):
@@ -317,9 +293,9 @@
                 spread(tile, False)
             if e == max(events - 2, 0):
                 for s in range(CUTS):
-                    own_piece_z(s)
+                    along(home_slot, s, has_up, has_down)
         for s in range(last):
-            own_piece_y(s)
+            cross(home_slot, s)
 
         back[...] = jnp.zeros_like(back)
         valence = layers * 4 * 2 * rows
@@ -328,18 +304,16 @@
         for e in range(-1, events):
             for xx in range(2):
                 tile = tile_of(source[e] if e >= 0 else z, across, xx)
-                ref = lines(tile, half)
-                got(ref, trial_recv.at[tile])
-                hand(ref, tile)
+                got(lines(tile, half), trial_recv.at[tile])
+                hand(tile)
 
         ref = psi_half(psi.at[1], half)
         got(ref, psi_recv.at[0])
-        send(ref, ref, psi_recv.at[1], me, other, psi_half(psi.at[1], 0))
-        along(came(mate_slot, last), mate_slot, last, has_up, has_down)
-        for e in range(events):
-            arrive_if(e, 1)
-        for tile in range(layers * 4):
-            got(lines(tile, other), hand_recv.at[tile])
+        send(ref, ref, POINTS, psi_recv.at[1], me, other)
+        came(mate_slot, last)
+        along(mate_slot, last, has_up, has_down)
+        arrive(1, 0, CUTS)
+        got(whole.at[pl.ds(0, layers * 4 * rows), :], hand_recv.at[0])
 
     wide = 256
 
@@ -359,33 +333,37 @@
         psi_t[1] = psi[1].reshape(valence, points).T
         project(1)
 
+    farthest = layers - 1
+
     def receive(i):
         kind, e = order[i]
         if kind == "z" and e > 0:
-            for late in range(e, events):
-                arrive_if(late, e + 1)
+            arrive(e + 1, last if e + 1 == farthest else 0, CUTS)
         if kind == "y":
             for s in range(last):
                 came(turns[i], s)
-        load_own[i].wait()
+
+    def between(i):
+        if i + 1 < slots and order[i + 1] == ("z", farthest - 1) and farthest > 1:
+            arrive(farthest, 0, last)
 
     def step(p, share, slot):
-        block = panel.at[slot]
+        block = block_of(slot)
         pair = jnp.dot(flat[p], block[...], preferred_element_type=f32)
         weighted = (share.astype(f32) * pair).astype(bf16)
         for h in range(2):
             back[p, h] += back_product(weighted, block[pl.ds(h * middle, middle), :])
 
+    pltpu.make_async_copy(screened_own, screened_own, local_sem.at[4]).wait()
+
     def use(k, carry):
         slot = turns[0]
         for i in range(final):
             slot = jnp.where(k == i, turns[i], slot)
-
-            @pl.when(k == i)
-            def _(i=i):
-                receive(i)
-
+            pl.when(k == i)(functools.partial(receive, i))
         step(0, screened_own[k], slot)
+        for i in range(final):
+            pl.when(k == i)(functools.partial(between, i))
         got(screened_in.at[k], screened_recv.at[k])
         step(1, screened_in[k], slot)
         return carry
@@ -402,14 +380,7 @@
     def swap(p):
         for kind in range(2):
             give[kind, p] = back[p, other, :, span(kind)].astype(bf16)
-            send(
-                give.at[kind, p],
-                take.at[kind, p],
-                take_recv.at[kind, p],
-                me,
-                other,
-                give.at[0, 0],
-            )
+            send(give.at[kind, p], take.at[kind, p], GIVE, take_recv.at[kind, p], me, other)
 
     def split(kind, p):
         got(take.at[kind, p], take_recv.at[kind, p])
@@ -435,37 +406,22 @@
             total = value if total is None else total + value
         return total.reshape(share, 2, block_rows, part)
 
-    settled = [0]
-
-    def settle(upto):
-        for i in range(settled[0], upto):
-            like, *conds = pending[i]
-            wait = remote(like, like, sends.at[i], parts_recv.at[0, 0, 0], me, other).wait_send
-            conds = [cond for cond in conds if cond is not None]
-            if conds:
-                pl.when(functools.reduce(jnp.logical_and, conds))(wait)
-            else:
-                wait()
-        settled[0] = upto
-
     mates = [mate_x, mate_y]
     homes, aways = [x, y], [aside, across]
+    with jax.named_scope("plast"):
+        swap(0)
+        got(screened_in.at[final], screened_recv.at[final])
+        step(1, screened_in[final], turns[final])
+        swap(1)
+
     with jax.named_scope("pearly"):
-        swap(0)
         for kind in range(2):
             split(kind, 0)
         for sub in range(SUBS):
             for kind in range(2):
-                keep[kind, sub] = product(0, kind, homes[kind], sub)
                 leave[kind, sub] = product(0, kind, aways[kind], sub)
 
-    with jax.named_scope("plast"):
-        got(screened_in.at[final], screened_recv.at[final])
-        step(1, screened_in[final], turns[final])
-
-    earlier = len(pending)
     with jax.named_scope("pfin"):
-        swap(1)
         for sub in range(SUBS):
             for kind in range(2):
                 if sub == 0:
@@ -475,17 +431,16 @@
                 send(
                     first_send.at[kind, sub],
                     first_got.at[kind, sub],
+                    FIRST,
                     first_recv.at[kind, sub],
                     mates[kind],
                     half,
-                    first_send.at[0, 0],
                 )
         for sub in range(SUBS):
             for kind in range(2):
-                keep[kind, sub] += product(1, kind, homes[kind], sub)
-
-    with jax.named_scope("psettle"):
-        settle(earlier)
+                home = homes[kind]
+                value = product(0, kind, home, sub) + product(1, kind, home, sub)
+                keep[kind, sub] = value
 
     with jax.named_scope("psecond"):
         for sub in range(SUBS):
@@ -502,10 +457,10 @@
                 send(
                     second_send.at[kind, sub],
                     second_got.at[kind, sub],
+                    SECOND,
                     second_recv.at[kind, sub],
                     mates[1 - kind],
                     half,
-                    second_send.at[0, 0],
                 )
                 keep[kind, sub, :, pl.ds(home, 1)] = summed(home).reshape(
                     share, 1, block_rows, part
@@ -525,11 +480,11 @@
                     for v in range(2):
                         send(
                             third.at[kind, sub, i, pl.ds(v * rows, rows)],
-                            parts.at[z, half, kind],
-                            parts_recv.at[z, half, kind],
+                            parts.at[half, kind, z],
+                            THIRD,
+                            parts_recv.at[half, kind],
                             tile_of(zz, y, x),
                             v,
-                            parts.at[0, 0, 0],
                             (z != zz) | (half != v),
                         )
 
@@ -543,30 +498,40 @@
                     value = keep[
                         kind, z // share, lax.rem(z, share), home, pl.ds(half * rows, rows)
                     ]
-                for d in range(layers):
-                    if flip == 0 and d == 0:
-                        continue
-                    zz = lax.rem(z + d, layers)
-                    got(parts.at[zz, vec, kind], parts_recv.at[zz, vec, kind])
-                    more = parts[zz, vec, kind].astype(f32)
+                count = layers - 1 + flip
+                got(parts.at[vec, kind, pl.ds(0, count)], parts_recv.at[vec, kind])
+                for d in range(1 - flip, layers):
+                    more = parts[vec, kind, lax.rem(z + d, layers)].astype(f32)
                     value = more if value is None else value + more
                 block = pl.ds(pl.multiple_of(vec * middle + kind * part, 128), part)
                 result[:, block] = value
-                load(result.at[:, block], out_hbm.at[:, block])
-
-    assert len(pending) <= sends.shape[0]
-    settle(len(pending))
-    for copy in local[-4:]:
-        copy.wait()
-
-
-def sends_of(layers):
-    events = layers - 1
-    slots = layers * 2
-    count = 1 + 2 * (events + 2) + 1 + 3 * CUTS + slots
-    count += events * 4 + layers * 2 + 1
-    count += 2 + (3 * CUTS + 2) * sum(events - e for e in range(events))
-    return count + 4 + 2 * SUBS * 2 + 2 * layers * 2
+
+    def rows_as(count):
+        return whole.at[pl.ds(0, count), :]
+
+    def pieces_as(count):
+        return panel.at[pl.ds(0, count * height), :]
+
+    with jax.named_scope("pend"):
+        sent(rows_as((8 * layers - 1) * rows), ROWS)
+        sent(pieces_as(CUTS + events * last), ACROSS)
+        for k in range(layers):
+            ends = (k == 0) + (k == layers - 1)
+            onward = sum((o < k < layers - 1) or (0 < k < o) for o in table[k])
+            count = (2 - ends + onward) * (CUTS + 1)
+            pl.when(z == k)(functools.partial(sent, pieces_as(count), LAYERS))
+        sent(screened_out, SHARE)
+        sent(psi.at[1], POINTS)
+        sent(give, GIVE)
+        sent(first_send, FIRST)
+        sent(second_send, SECOND)
+        sent(rows_as(2 * (2 * layers - 1) * rows * part // conduct), THIRD)
+
+
+def write_out(result, out_hbm, sem):
+    copy = pltpu.make_async_copy(result, out_hbm, sem)
+    copy.start()
+    copy.wait()
 
 
 def fused(tiles, trial, psi_v, psi_c, screened):
@@ -584,11 +549,10 @@
     vmem = pltpu.VMEM
     out = pl.pallas_call(
         functools.partial(body, layers),
-        out_shape=jax.ShapeDtypeStruct((rows, conduct), f32),
+        out_shape=vmem((rows, conduct), f32),
         in_specs=[far] * 4,
-        out_specs=far,
+        out_specs=pl.BlockSpec(memory_space=vmem),
         scratch_shapes=[
-            vmem((rows, conduct), f32),
             vmem((valence, conduct), bf16),
             vmem((2, layers, 2, 2, 2 * rows, points), bf16),
             vmem((2, points, valence), bf16),
@@ -596,7 +560,7 @@
             vmem((slots, points, width), f32),
             vmem((slots, points, width), bf16),
             vmem((slots, points, width), bf16),
-            vmem((slots, conduct, width), bf16),
+            vmem((slots * conduct, width), bf16),
             vmem((2, points, conduct), bf16),
             vmem((2, 2, points, middle), f32),
             vmem((2, 2, points, part), bf16),
@@ -608,18 +572,18 @@
             vmem((2, SUBS, share, 2 * rows, part), bf16),
             vmem((2, SUBS, share, 2 * rows, part), bf16),
             vmem((2, SUBS, share, 2 * rows, part), bf16),
-            vmem((layers, 2, 2, rows, part), bf16),
-            dma((3 + 2 * slots + 4,)),
-            dma((sends_of(layers),)),
+            vmem((2, 2, layers, rows, part), bf16),
+            dma((5,)),
+            dma((9,)),
             dma((tiles,)),
-            dma((tiles,)),
+            dma((1,)),
             dma((2,)),
             dma((slots,)),
             dma((slots, CUTS)),
             dma((2, 2)),
             dma((2, SUBS)),
             dma((2, SUBS)),
-            dma((layers, 2, 2)),
+            dma((2, 2)),
         ],
         compiler_params=pltpu.CompilerParams(
             collective_id=0, has_side_effects=True, vmem_limit_bytes=58 * 1024 * 1024
@@ -630,6 +594,14 @@
         psi_c[:, 0, :],
         screened,
     )
+    out = pl.pallas_call(
+        write_out,
+        out_shape=jax.ShapeDtypeStruct((rows, conduct), f32),
+        in_specs=[pl.BlockSpec(memory_space=vmem)],
+        out_specs=far,
+        scratch_shapes=[dma(())],
+        compiler_params=pltpu.CompilerParams(vmem_limit_bytes=1024 * 1024),
+    )(out)
     return out[None]
 
 

time: 92.7 us -> 86.5 us (0.933)
  Pallas kernels: 91 us -> 86.3 us
  local copies, waits for them, and re-layouts: 1.57 us -> 0 us
    pallas_call x1 -> x2, Pallas kernels: 91 us -> 86.3 us  [the longest x1 85.6 us: fused(): pl.pallas_call(functools.partial(body, layers), out_shape=vmem((rows, con...]
    unnamed x1 -> x0, local copies, waits for them, and re-layouts: 1.57 us -> none
where the time goes in v5:
time: 86.5 us; the launch traced here: 86.3 us
  Pallas kernels  86.3 us (100%)
    pallas_call x1, Pallas kernels, fused(): pl.pallas_call(functools.partial(body, layers), out_shape=vmem((rows, con...  85.6 us

profile of v5, /device:TPU:0, one launch (start us, length us, event | category | flops | bytes accessed | tf_op | source)
XLA Modules:
  0.0 86.3 jit_solution(492260627936810728)
XLA Ops:
  0.0 85.6 %shard_map.46.result = f32[32,1024]{1,0:T(8,128)S(1)} custom-call(bf16[32,1024]{1,0:T(8,128)(2,1)} %bitcast.6, bf16[4,2,2,64,512]{4,3,2,1,0:T(8,128)(2,1)} %bitcast.4, bf16[1024,256]{1,0:T(8,128)(2,1)} %bitcast.5, f32[512,4096]{1,0:T(8,128)} %screened_hbm.1), custom_call_target="tpu_custom_call" | custom-call | tf_op jit(solution)/shard_map/pallas_call | solution.py:550
  85.6 0.7 shard_map.47

commit v6 on v5

--- a/solution.py
+++ b/solution.py
@@ -8,7 +8,7 @@
 from jax.sharding import PartitionSpec as P
 
 CUTS = 4
-SUBS = 2
+AHEAD = 2
 ROWS, ACROSS, LAYERS, SHARE, POINTS, GIVE, FIRST, SECOND, THIRD = range(9)
 
 
@@ -57,6 +57,10 @@
     ]
 
 
+def outer_first(layers):
+    return sorted(range(layers), key=lambda k: (-abs(2 * k - layers + 1), k))
+
+
 def pick(values, at):
     chosen = jnp.int32(values[0])
     for k, value in enumerate(values[1:], 1):
@@ -86,7 +90,6 @@
     first_send,
     first_got,
     keep,
-    leave,
     second_send,
     second_got,
     third,
@@ -116,6 +119,11 @@
     distance = [pick([abs(row[e] - k) for k, row in enumerate(table)], z) for e in range(events)]
     at_distance = [[distance[e] == k for k in range(layers)] for e in range(events)]
 
+    ranks = outer_first(layers)
+
+    def place_of(zz):
+        return pick([ranks.index(k) for k in range(layers)], zz)
+
     def tile_of(zz, yy, xx):
         return zz * 4 + yy * 2 + xx
 
@@ -148,6 +156,7 @@
     height = psi_c_hbm.shape[0] // CUTS
 
     def lines(tile, vec):
+        tile = place_of(tile // 4) * 4 + tile % 4
         start = pl.multiple_of((tile * 2 + vec) * rows, rows)
         return whole.at[pl.ds(start, rows), :]
 
@@ -165,7 +174,8 @@
         return panel.at[pl.ds(pl.multiple_of(slot * conduct, conduct), conduct), :]
 
     load_rows = load(trial_hbm, lines(me, half), 0)
-    load_psi = load(psi_v_hbm, psi.at[0], 1)
+    for i, layer in enumerate(ranks):
+        load(psi_v_hbm.at[layer], psi.at[0, i], 1)
     load_block = load(psi_c_hbm, block_of(home_slot), 2)
 
     def remote(src, dst, send, recv, tile, vec):
@@ -272,7 +282,7 @@
             load(screened_hbm.at[:, columns(turn * 2 + aside)], stage.at[i], 3)
         for i, turn in enumerate(turns):
             load(screened_hbm.at[:, columns(turn * 2 + x)], screened_own.at[i], 4)
-        load_psi.wait()
+        pltpu.make_async_copy(psi_v_hbm, psi.at[0], local_sem.at[1]).wait()
         ref = psi_half(psi.at[0], half)
         send(ref, psi_half(psi.at[1], half), POINTS, psi_recv.at[0], mate_x, half)
         got(lines(mate_x, half), trial_recv.at[mate_x])
@@ -347,12 +357,17 @@
         if i + 1 < slots and order[i + 1] == ("z", farthest - 1) and farthest > 1:
             arrive(farthest, 0, last)
 
-    def step(p, share, slot):
+    def step(p, share, slot, ready=None, between=None):
         block = block_of(slot)
         pair = jnp.dot(flat[p], block[...], preferred_element_type=f32)
-        weighted = (share.astype(f32) * pair).astype(bf16)
-        for h in range(2):
-            back[p, h] += back_product(weighted, block[pl.ds(h * middle, middle), :])
+        if ready is not None:
+            ready()
+        weighted = (share().astype(f32) * pair).astype(bf16)
+        for h in (other, half):
+            rows_of = pl.ds(pl.multiple_of(h * middle, middle), middle)
+            back[p, h] += back_product(weighted, block[rows_of, :])
+            if between is not None and h is other:
+                between()
 
     pltpu.make_async_copy(screened_own, screened_own, local_sem.at[4]).wait()
 
@@ -361,18 +376,18 @@
         for i in range(final):
             slot = jnp.where(k == i, turns[i], slot)
             pl.when(k == i)(functools.partial(receive, i))
-        step(0, screened_own[k], slot)
+        step(0, lambda: screened_own[k], slot)
         for i in range(final):
             pl.when(k == i)(functools.partial(between, i))
         got(screened_in.at[k], screened_recv.at[k])
-        step(1, screened_in[k], slot)
+        step(1, lambda: screened_in[k], slot)
         return carry
 
     final = slots - 1
     with jax.named_scope("puse"):
         lax.fori_loop(0, final, use, 0)
         receive(final)
-        step(0, screened_own[final], turns[final])
+        step(0, lambda: screened_own[final], turns[final])
 
     def span(kind):
         return pl.ds(kind * part, part)
@@ -390,103 +405,89 @@
         low = (total - high.astype(f32)).astype(bf16)
         flat[p, :, pl.ds(middle + kind * part, part)] = low
 
-    share = layers // SUBS
     block_rows = 2 * rows
 
-    def product(p, kind, at, sub):
-        if kind == 0:
-            left = psi[p, pl.ds(sub * share, share), :, pl.ds(at, 1)]
-        else:
-            left = psi[p, pl.ds(sub * share, share), pl.ds(at, 1)]
-        left = left.reshape(share * 2 * block_rows, points)
+    def product(p, kind, i):
+        left = psi[p, i].reshape(4 * block_rows, points)
         total = None
         for level in range(2):
             cols = pl.ds(level * middle + kind * part, part)
             value = jnp.dot(left, flat[p, :, cols], preferred_element_type=f32)
             total = value if total is None else total + value
-        return total.reshape(share, 2, block_rows, part)
-
-    mates = [mate_x, mate_y]
-    homes, aways = [x, y], [aside, across]
+        return total.reshape(2, 2, block_rows, part)
+
+    def leave(i, kind):
+        if i < AHEAD:
+            keep[kind, i] += product(1, kind, i)
+        else:
+            keep[kind, i] = product(0, kind, i) + product(1, kind, i)
+        if kind == 0:
+            away = keep[kind, i, :, pl.ds(aside, 1)]
+        else:
+            away = keep[kind, i, pl.ds(across, 1)]
+        first_send[kind, i] = away.reshape(2, block_rows, part).astype(bf16)
+        ref = first_send.at[kind, i]
+        recv = first_recv.at[kind, i]
+        send(ref, first_got.at[kind, i], FIRST, recv, [mate_x, mate_y][kind], half)
+
+    def again(i, kind):
+        got(first_got.at[kind, i], first_recv.at[kind, i])
+        yy, xx = [(across, x), (y, aside)][kind]
+        away = [across, aside][kind]
+        value = keep[kind, i, yy, xx] + first_got[kind, i, away].astype(f32)
+        second_send[kind, i] = value.astype(bf16)
+        ref = second_send.at[kind, i]
+        recv = second_recv.at[kind, i]
+        send(ref, second_got.at[kind, i], SECOND, recv, [mate_y, mate_x][kind], half)
+        keep[kind, i, y, x] += first_got[kind, i, [y, x][kind]].astype(f32)
+
+    def deliver(i, kind):
+        got(second_got.at[kind, i], second_recv.at[kind, i])
+        value = keep[kind, i, y, x] + second_got[kind, i].astype(f32)
+        keep[kind, i, y, x] = value
+        third[kind, i] = value.astype(bf16)
+        layer = ranks[i]
+        for v in range(2):
+            send(
+                third.at[kind, i, pl.ds(v * rows, rows)],
+                parts.at[half, kind, z],
+                THIRD,
+                parts_recv.at[half, kind],
+                tile_of(layer, y, x),
+                v,
+                (z != layer) | (half != v),
+            )
+
     with jax.named_scope("plast"):
         swap(0)
-        got(screened_in.at[final], screened_recv.at[final])
-        step(1, screened_in[final], turns[final])
-        swap(1)
+        step(
+            1,
+            lambda: screened_in[final],
+            turns[final],
+            lambda: got(screened_in.at[final], screened_recv.at[final]),
+            lambda: swap(1),
+        )
 
     with jax.named_scope("pearly"):
         for kind in range(2):
             split(kind, 0)
-        for sub in range(SUBS):
+        for i in range(AHEAD):
             for kind in range(2):
-                leave[kind, sub] = product(0, kind, aways[kind], sub)
-
-    with jax.named_scope("pfin"):
-        for sub in range(SUBS):
+                keep[kind, i] = product(0, kind, i)
+
+    with jax.named_scope("preduce"):
+        for i in range(layers + 2):
             for kind in range(2):
-                if sub == 0:
+                if i == 0:
                     split(kind, 1)
-                value = leave[kind, sub] + product(1, kind, aways[kind], sub)
-                first_send[kind, sub] = value.astype(bf16)
-                send(
-                    first_send.at[kind, sub],
-                    first_got.at[kind, sub],
-                    FIRST,
-                    first_recv.at[kind, sub],
-                    mates[kind],
-                    half,
-                )
-        for sub in range(SUBS):
+                if i < layers:
+                    leave(i, kind)
             for kind in range(2):
-                home = homes[kind]
-                value = product(0, kind, home, sub) + product(1, kind, home, sub)
-                keep[kind, sub] = value
-
-    with jax.named_scope("psecond"):
-        for sub in range(SUBS):
+                if 0 <= i - 1 < layers:
+                    again(i - 1, kind)
             for kind in range(2):
-                got(first_got.at[kind, sub], first_recv.at[kind, sub])
-                away, home = [(across, y), (aside, x)][kind]
-
-                def summed(at, kind=kind, sub=sub):
-                    mine = keep[kind, sub, :, pl.ds(at, 1)]
-                    theirs = first_got[kind, sub, :, pl.ds(at, 1)].astype(f32)
-                    return (mine + theirs).reshape(share, block_rows, part)
-
-                second_send[kind, sub] = summed(away).astype(bf16)
-                send(
-                    second_send.at[kind, sub],
-                    second_got.at[kind, sub],
-                    SECOND,
-                    second_recv.at[kind, sub],
-                    mates[1 - kind],
-                    half,
-                )
-                keep[kind, sub, :, pl.ds(home, 1)] = summed(home).reshape(
-                    share, 1, block_rows, part
-                )
-
-    with jax.named_scope("pthird"):
-        for sub in range(SUBS):
-            for kind in range(2):
-                got(second_got.at[kind, sub], second_recv.at[kind, sub])
-                home = [y, x][kind]
-                mine = keep[kind, sub, :, pl.ds(home, 1)].reshape(share, block_rows, part)
-                value = mine + second_got[kind, sub].astype(f32)
-                keep[kind, sub, :, pl.ds(home, 1)] = value.reshape(share, 1, block_rows, part)
-                third[kind, sub] = value.astype(bf16)
-                for i in range(share):
-                    zz = sub * share + i
-                    for v in range(2):
-                        send(
-                            third.at[kind, sub, i, pl.ds(v * rows, rows)],
-                            parts.at[half, kind, z],
-                            THIRD,
-                            parts_recv.at[half, kind],
-                            tile_of(zz, y, x),
-                            v,
-                            (z != zz) | (half != v),
-                        )
+                if 0 <= i - 2 < layers:
+                    deliver(i - 2, kind)
 
     with jax.named_scope("psum"):
         for flip in range(2):
@@ -494,10 +495,8 @@
             for kind in range(2):
                 value = None
                 if flip == 0:
-                    home = [y, x][kind]
-                    value = keep[
-                        kind, z // share, lax.rem(z, share), home, pl.ds(half * rows, rows)
-                    ]
+                    mine = pl.ds(pl.multiple_of(half * rows, rows), rows)
+                    value = keep[kind, place_of(z), y, x, mine]
                 count = layers - 1 + flip
                 got(parts.at[vec, kind, pl.ds(0, count)], parts_recv.at[vec, kind])
                 for d in range(1 - flip, layers):
@@ -542,7 +541,6 @@
     part = middle // 2
     layers = tiles // 4
     slots = layers * 2
-    share = layers // SUBS
     bf16, f32 = jnp.bfloat16, jnp.float32
     far = pl.BlockSpec(memory_space=pl.ANY)
     dma = pltpu.SemaphoreType.DMA
@@ -565,13 +563,12 @@
             vmem((2, 2, points, middle), f32),
             vmem((2, 2, points, part), bf16),
             vmem((2, 2, points, part), bf16),
-            vmem((2, SUBS, share, 2, 2 * rows, part), bf16),
-            vmem((2, SUBS, share, 2, 2 * rows, part), bf16),
-            vmem((2, SUBS, share, 2, 2 * rows, part), f32),
-            vmem((2, SUBS, share, 2, 2 * rows, part), f32),
-            vmem((2, SUBS, share, 2 * rows, part), bf16),
-            vmem((2, SUBS, share, 2 * rows, part), bf16),
-            vmem((2, SUBS, share, 2 * rows, part), bf16),
+            vmem((2, layers, 2, 2 * rows, part), bf16),
+            vmem((2, layers, 2, 2 * rows, part), bf16),
+            vmem((2, layers, 2, 2, 2 * rows, part), f32),
+            vmem((2, layers, 2 * rows, part), bf16),
+            vmem((2, layers, 2 * rows, part), bf16),
+            vmem((2, layers, 2 * rows, part), bf16),
             vmem((2, 2, layers, rows, part), bf16),
             dma((5,)),
             dma((9,)),
@@ -581,8 +578,8 @@
             dma((slots,)),
             dma((slots, CUTS)),
             dma((2, 2)),
-            dma((2, SUBS)),
-            dma((2, SUBS)),
+            dma((2, layers)),
+            dma((2, layers)),
             dma((2, 2)),
         ],
         compiler_params=pltpu.CompilerParams(
@@ -612,7 +609,7 @@
         fits = (
             trial.shape[0] == 1
             and mesh.shape["vec"] == 2
-            and tiles % (4 * SUBS) == 0
+            and tiles % 8 == 0
             and psi_v.shape[1] % 128 == 0
             and psi_c.shape[2] % 128 == 0
             and trial.shape[1] % 16 == 0

time: 86.5 us -> 86.1 us (level)
  no operation moved by 1% of the time
where the time goes in v6:
time: 86.1 us; the launch traced here: 86 us
  Pallas kernels  86 us (100%)
    pallas_call x1, Pallas kernels, fused(): pl.pallas_call(functools.partial(body, layers), out_shape=vmem((rows, con...  85.3 us

profile of v6, /device:TPU:0, one launch (start us, length us, event | category | flops | bytes accessed | tf_op | source)
XLA Modules:
  0.0 86.0 jit_solution(111335327460515003)
XLA Ops:
  0.0 85.3 %shard_map.46.result = f32[32,1024]{1,0:T(8,128)S(1)} custom-call(bf16[32,1024]{1,0:T(8,128)(2,1)} %bitcast.6, bf16[4,2,2,64,512]{4,3,2,1,0:T(8,128)(2,1)} %bitcast.4, bf16[1024,256]{1,0:T(8,128)(2,1)} %bitcast.5, f32[512,4096]{1,0:T(8,128)} %screened_hbm.1), custom_call_target="tpu_custom_call" | custom-call | tf_op jit(solution)/shard_map/pallas_call | solution.py:548
  85.3 0.7 shard_map.47

commit v7 on v6

--- a/solution.py
+++ b/solution.py
@@ -130,6 +130,7 @@
     mate_x, mate_y = tile_of(z, y, aside), tile_of(z, across, x)
     up, down = jnp.minimum(z + 1, layers - 1), jnp.maximum(z - 1, 0)
     has_up, has_down = z < layers - 1, z > 0
+    at_end = (z == 0) | (z == layers - 1)
     on_up = [has_up & (source[e] < z) for e in range(events)]
     on_down = [has_down & (source[e] > z) for e in range(events)]
 
@@ -188,17 +189,24 @@
             device_id_type=pl.DeviceIdType.MESH,
         )
 
-    partners = [(mate_x, half), (mate_y, half), (me, other)]
-    for d in range(1, layers):
-        for v in range(2):
-            partners.append((tile_of(lax.rem(z + d, layers), y, x), v))
+    partners = [(mate_x, half, None), (mate_y, half, None), (me, other, None)]
+    partners += [(tile_of(up, y, x), half, has_up), (tile_of(down, y, x), half, has_down)]
     with jax.named_scope("pbar"):
         barrier = pltpu.get_barrier_semaphore()
-        for partner in partners:
+
+        def greet(tile, vec):
             pl.semaphore_signal(
-                barrier, inc=1, device_id=partner, device_id_type=pl.DeviceIdType.MESH
+                barrier, inc=1, device_id=(tile, vec), device_id_type=pl.DeviceIdType.MESH
             )
-        pl.semaphore_wait(barrier, len(partners))
+
+        for tile, vec, cond in partners:
+            if cond is None:
+                greet(tile, vec)
+            else:
+                pl.when(cond)(functools.partial(greet, tile, vec))
+        for k in range(layers):
+            count = 3 + (k > 0) + (k < layers - 1)
+            pl.when(z == k)(functools.partial(pl.semaphore_wait, barrier, count))
 
     def send(src, dst, group, recv, tile, vec, cond=None):
         copy = remote(src, dst, sends.at[group], recv, tile, vec)
@@ -221,12 +229,11 @@
         ref = lines(tile, half)
         send(ref, ref, ROWS, hand_recv.at[0], me, other)
 
-    def spread(tile, column):
+    def spread(tile, to_up, to_down):
         ref = lines(tile, half)
         recv = trial_recv.at[tile]
-        if column:
-            for e in range(events):
-                send(ref, ref, ROWS, recv, tile_of(source[e], y, x), half)
+        send(ref, ref, ROWS, recv, tile_of(up, y, x), half, to_up)
+        send(ref, ref, ROWS, recv, tile_of(down, y, x), half, to_down)
         send(ref, ref, ROWS, recv, mate_y, half)
         hand(tile)
 
@@ -277,7 +284,7 @@
         ref = lines(me, half)
         load_rows.wait()
         send(ref, ref, ROWS, trial_recv.at[me], mate_x, half)
-        spread(me, True)
+        spread(me, has_up, has_down)
         for i, turn in enumerate(turns):
             load(screened_hbm.at[:, columns(turn * 2 + aside)], stage.at[i], 3)
         for i, turn in enumerate(turns):
@@ -286,7 +293,7 @@
         ref = psi_half(psi.at[0], half)
         send(ref, psi_half(psi.at[1], half), POINTS, psi_recv.at[0], mate_x, half)
         got(lines(mate_x, half), trial_recv.at[mate_x])
-        spread(mate_x, True)
+        spread(mate_x, has_up, has_down)
         load_block.wait()
         cross(home_slot, last)
 
@@ -300,10 +307,15 @@
             for xx in range(2):
                 tile = tile_of(source[e], y, xx)
                 got(lines(tile, half), trial_recv.at[tile])
-                spread(tile, False)
-            if e == max(events - 2, 0):
+                spread(tile, on_up[e], on_down[e])
+            if e == events - 2:
                 for s in range(CUTS):
-                    along(home_slot, s, has_up, has_down)
+                    along(home_slot, s, has_up & at_end, has_down & at_end)
+        for s in range(CUTS):
+            if events > 1:
+                along(home_slot, s, has_up & ~at_end, has_down & ~at_end)
+            else:
+                along(home_slot, s, has_up, has_down)
         for s in range(last):
             cross(home_slot, s)
 
@@ -416,19 +428,24 @@
             total = value if total is None else total + value
         return total.reshape(2, 2, block_rows, part)
 
-    def leave(i, kind):
-        if i < AHEAD:
-            keep[kind, i] += product(1, kind, i)
-        else:
-            keep[kind, i] = product(0, kind, i) + product(1, kind, i)
-        if kind == 0:
-            away = keep[kind, i, :, pl.ds(aside, 1)]
-        else:
-            away = keep[kind, i, pl.ds(across, 1)]
-        first_send[kind, i] = away.reshape(2, block_rows, part).astype(bf16)
-        ref = first_send.at[kind, i]
-        recv = first_recv.at[kind, i]
-        send(ref, first_got.at[kind, i], FIRST, recv, [mate_x, mate_y][kind], half)
+    def prepare(i):
+        for kind in range(2):
+            if i < AHEAD:
+                keep[kind, i] += product(1, kind, i)
+            else:
+                keep[kind, i] = product(0, kind, i) + product(1, kind, i)
+        for kind in range(2):
+            if kind == 0:
+                away = keep[kind, i, :, pl.ds(aside, 1)]
+            else:
+                away = keep[kind, i, pl.ds(across, 1)]
+            first_send[kind, i] = away.reshape(2, block_rows, part).astype(bf16)
+
+    def leave(i):
+        for kind in range(2):
+            ref = first_send.at[kind, i]
+            recv = first_recv.at[kind, i]
+            send(ref, first_got.at[kind, i], FIRST, recv, [mate_x, mate_y][kind], half)
 
     def again(i, kind):
         got(first_got.at[kind, i], first_recv.at[kind, i])
@@ -476,18 +493,24 @@
                 keep[kind, i] = product(0, kind, i)
 
     with jax.named_scope("preduce"):
-        for i in range(layers + 2):
+        for kind in range(2):
+            split(kind, 1)
+        prepare(0)
+        leave(0)
+        prepare(1)
+        leave(1)
+        for i in range(layers):
+            if i + 2 < layers:
+                prepare(i + 2)
             for kind in range(2):
-                if i == 0:
-                    split(kind, 1)
-                if i < layers:
-                    leave(i, kind)
-            for kind in range(2):
-                if 0 <= i - 1 < layers:
-                    again(i - 1, kind)
-            for kind in range(2):
-                if 0 <= i - 2 < layers:
-                    deliver(i - 2, kind)
+                again(i, kind)
+            if i + 2 < layers:
+                leave(i + 2)
+            if i > 0:
+                for kind in range(2):
+                    deliver(i - 1, kind)
+        for kind in range(2):
+            deliver(layers - 1, kind)
 
     with jax.named_scope("psum"):
         for flip in range(2):
@@ -506,19 +529,20 @@
                 result[:, block] = value
 
     def rows_as(count):
-        return whole.at[pl.ds(0, count), :]
+        return panel.at[pl.ds(0, count * conduct // width), :]
 
     def pieces_as(count):
         return panel.at[pl.ds(0, count * height), :]
 
     with jax.named_scope("pend"):
-        sent(rows_as((8 * layers - 1) * rows), ROWS)
         sent(pieces_as(CUTS + events * last), ACROSS)
         for k in range(layers):
             ends = (k == 0) + (k == layers - 1)
             onward = sum((o < k < layers - 1) or (0 < k < o) for o in table[k])
             count = (2 - ends + onward) * (CUTS + 1)
             pl.when(z == k)(functools.partial(sent, pieces_as(count), LAYERS))
+            count = 1 + 2 * (2 - ends + 2) + 2 * (2 * events + onward) + 2 * layers
+            pl.when(z == k)(functools.partial(sent, rows_as(count * rows), ROWS))
         sent(screened_out, SHARE)
         sent(psi.at[1], POINTS)
         sent(give, GIVE)

time: 86.1 us -> 85.4 us (level)
  no operation moved by 1% of the time
where the time goes in v7:
time: 85.4 us; the launch traced here: 85.2 us
  Pallas kernels  85.2 us (100%)
    pallas_call x1, Pallas kernels, fused(): pl.pallas_call(functools.partial(body, layers), out_shape=vmem((rows, con...  84.6 us

profile of v7, /device:TPU:0, one launch (start us, length us, event | category | flops | bytes accessed | tf_op | source)
XLA Modules:
  0.0 85.2 jit_solution(5306888629535509303)
XLA Ops:
  0.0 84.6 %shard_map.46.result = f32[32,1024]{1,0:T(8,128)S(1)} custom-call(bf16[32,1024]{1,0:T(8,128)(2,1)} %bitcast.6, bf16[4,2,2,64,512]{4,3,2,1,0:T(8,128)(2,1)} %bitcast.4, bf16[1024,256]{1,0:T(8,128)(2,1)} %bitcast.5, f32[512,4096]{1,0:T(8,128)} %screened_hbm.1), custom_call_target="tpu_custom_call" | custom-call | tf_op jit(solution)/shard_map/pallas_call | solution.py:572
  84.6 0.7 shard_map.47

commit v8 on v7

--- a/solution.py
+++ b/solution.py
@@ -309,14 +309,19 @@
                 got(lines(tile, half), trial_recv.at[tile])
                 spread(tile, on_up[e], on_down[e])
             if e == events - 2:
+                cross(home_slot, 0)
                 for s in range(CUTS):
-                    along(home_slot, s, has_up & at_end, has_down & at_end)
-        for s in range(CUTS):
-            if events > 1:
+                    if s < CUTS // 2:
+                        along(home_slot, s, has_up, has_down)
+                    else:
+                        along(home_slot, s, has_up & at_end, has_down & at_end)
+        if events > 1:
+            for s in range(CUTS // 2, CUTS):
                 along(home_slot, s, has_up & ~at_end, has_down & ~at_end)
-            else:
+        else:
+            for s in range(CUTS):
                 along(home_slot, s, has_up, has_down)
-        for s in range(last):
+        for s in range(1 if events > 1 else 0, last):
             cross(home_slot, s)
 
         back[...] = jnp.zeros_like(back)
@@ -495,17 +500,16 @@
     with jax.named_scope("preduce"):
         for kind in range(2):
             split(kind, 1)
-        prepare(0)
-        leave(0)
-        prepare(1)
-        leave(1)
+        lead = layers - 1
+        for i in range(lead):
+            prepare(i)
+            leave(i)
+        prepare(lead)
         for i in range(layers):
-            if i + 2 < layers:
-                prepare(i + 2)
             for kind in range(2):
                 again(i, kind)
-            if i + 2 < layers:
-                leave(i + 2)
+            if i == 0:
+                leave(lead)
             if i > 0:
                 for kind in range(2):
                     deliver(i - 1, kind)

time: 85.4 us -> 82.3 us (0.964)
  Pallas kernels: 85.2 us -> 82.2 us
    pallas_call x1, Pallas kernels: 84.6 us -> 81.5 us  [fused(): pl.pallas_call(functools.partial(body, layers), out_shape=vmem((rows, con...]
where the time goes in v8:
time: 82.3 us; the launch traced here: 82.2 us
  Pallas kernels  82.2 us (100%)
    pallas_call x1, Pallas kernels, fused(): pl.pallas_call(functools.partial(body, layers), out_shape=vmem((rows, con...  81.5 us

profile of v8, /device:TPU:0, one launch (start us, length us, event | category | flops | bytes accessed | tf_op | source)
XLA Modules:
  0.0 82.2 jit_solution(1239130497023846603)
XLA Ops:
  0.0 81.5 %shard_map.46.result = f32[32,1024]{1,0:T(8,128)S(1)} custom-call(bf16[32,1024]{1,0:T(8,128)(2,1)} %bitcast.6, bf16[4,2,2,64,512]{4,3,2,1,0:T(8,128)(2,1)} %bitcast.4, bf16[1024,256]{1,0:T(8,128)(2,1)} %bitcast.5, f32[512,4096]{1,0:T(8,128)} %screened_hbm.1), custom_call_target="tpu_custom_call" | custom-call | tf_op jit(solution)/shard_map/pallas_call | solution.py:576
  81.5 0.7 shard_map.47

commit v9 on v8

--- a/solution.py
+++ b/solution.py
@@ -328,6 +328,9 @@
         valence = layers * 4 * 2 * rows
         psi_t[0] = psi[0].reshape(valence, points).T
 
+        came(mate_slot, last)
+        along(mate_slot, last, has_up, has_down)
+        arrive(1, 0, CUTS // 2)
         for e in range(-1, events):
             for xx in range(2):
                 tile = tile_of(source[e] if e >= 0 else z, across, xx)
@@ -337,9 +340,7 @@
         ref = psi_half(psi.at[1], half)
         got(ref, psi_recv.at[0])
         send(ref, ref, POINTS, psi_recv.at[1], me, other)
-        came(mate_slot, last)
-        along(mate_slot, last, has_up, has_down)
-        arrive(1, 0, CUTS)
+        arrive(1, CUTS // 2, CUTS)
         got(whole.at[pl.ds(0, layers * 4 * rows), :], hand_recv.at[0])
 
     wide = 256
@@ -360,31 +361,33 @@
         psi_t[1] = psi[1].reshape(valence, points).T
         project(1)
 
-    farthest = layers - 1
+    turn_of = {e + 1: i for i, (kind, e) in enumerate(order) if kind == "z" and e > 0}
 
     def receive(i):
         kind, e = order[i]
         if kind == "z" and e > 0:
-            arrive(e + 1, last if e + 1 == farthest else 0, CUTS)
+            arrive(e + 1, last, CUTS)
         if kind == "y":
             for s in range(last):
                 came(turns[i], s)
 
     def between(i):
-        if i + 1 < slots and order[i + 1] == ("z", farthest - 1) and farthest > 1:
-            arrive(farthest, 0, last)
-
-    def step(p, share, slot, ready=None, between=None):
+        for k, turn in turn_of.items():
+            if i == turn - 2:
+                arrive(k, 0, CUTS // 2)
+            if i == turn - 1:
+                arrive(k, CUTS // 2, last)
+
+    def step(p, share, slot, ready=None, done=None):
         block = block_of(slot)
         pair = jnp.dot(flat[p], block[...], preferred_element_type=f32)
         if ready is not None:
             ready()
         weighted = (share().astype(f32) * pair).astype(bf16)
-        for h in (other, half):
-            rows_of = pl.ds(pl.multiple_of(h * middle, middle), middle)
-            back[p, h] += back_product(weighted, block[rows_of, :])
-            if between is not None and h is other:
-                between()
+        for h in range(2):
+            back[p, h] += back_product(weighted, block[pl.ds(h * middle, middle), :])
+            if done is not None:
+                done(h)
 
     pltpu.make_async_copy(screened_own, screened_own, local_sem.at[4]).wait()
 
@@ -480,22 +483,26 @@
                 (z != layer) | (half != v),
             )
 
+    def early():
+        for kind in range(2):
+            split(kind, 0)
+        for i in range(AHEAD):
+            for kind in range(2):
+                keep[kind, i] = product(0, kind, i)
+
     with jax.named_scope("plast"):
         swap(0)
+        pl.when(half == 0)(early)
         step(
             1,
             lambda: screened_in[final],
             turns[final],
             lambda: got(screened_in.at[final], screened_recv.at[final]),
-            lambda: swap(1),
+            lambda h: pl.when(half != h)(functools.partial(swap, 1)),
         )
 
     with jax.named_scope("pearly"):
-        for kind in range(2):
-            split(kind, 0)
-        for i in range(AHEAD):
-            for kind in range(2):
-                keep[kind, i] = product(0, kind, i)
+        pl.when(half == 1)(early)
 
     with jax.named_scope("preduce"):
         for kind in range(2):

time: 82.3 us -> 82 us (level)
  no operation moved by 1% of the time
where the time goes in v9:
time: 82 us; the launch traced here: 81.9 us
  Pallas kernels  81.9 us (100%)
    pallas_call x1, Pallas kernels, fused(): pl.pallas_call(functools.partial(body, layers), out_shape=vmem((rows, con...  81.2 us

profile of v9, /device:TPU:0, one launch (start us, length us, event | category | flops | bytes accessed | tf_op | source)
XLA Modules:
  0.0 81.9 jit_solution(11395235734563758359)
XLA Ops:
  0.0 81.2 %shard_map.46.result = f32[32,1024]{1,0:T(8,128)S(1)} custom-call(bf16[32,1024]{1,0:T(8,128)(2,1)} %bitcast.6, bf16[4,2,2,64,512]{4,3,2,1,0:T(8,128)(2,1)} %bitcast.4, bf16[1024,256]{1,0:T(8,128)(2,1)} %bitcast.5, f32[512,4096]{1,0:T(8,128)} %screened_hbm.1), custom_call_target="tpu_custom_call" | custom-call | tf_op jit(solution)/shard_map/pallas_call | solution.py:583
  81.2 0.7 shard_map.47

commit v10 on v9

--- a/solution.py
+++ b/solution.py
@@ -84,12 +84,14 @@
     screened_in,
     panel,
     flat,
+    pair,
     back,
     give,
     take,
     first_send,
     first_got,
     keep,
+    final_sum,
     second_send,
     second_got,
     third,
@@ -138,6 +140,7 @@
         return zz * 2 + yy
 
     slots = layers * 2
+    final = slots - 1
     order = [("own", 0)]
     for e in range(events - 1):
         order += [("z", e), ("y", e - 1)]
@@ -157,8 +160,9 @@
     height = psi_c_hbm.shape[0] // CUTS
 
     def lines(tile, vec):
-        tile = place_of(tile // 4) * 4 + tile % 4
-        start = pl.multiple_of((tile * 2 + vec) * rows, rows)
+        place = place_of(tile // 4)
+        place = ((place // 2) * 2 + vec) * 2 + place % 2
+        start = pl.multiple_of((place * 4 + tile % 4) * rows, rows)
         return whole.at[pl.ds(start, rows), :]
 
     def columns(tile):
@@ -176,8 +180,12 @@
 
     load_rows = load(trial_hbm, lines(me, half), 0)
     for i, layer in enumerate(ranks):
-        load(psi_v_hbm.at[layer], psi.at[0, i], 1)
+        for v in range(2):
+            load(psi_v_hbm.at[layer, :, :, v], psi.at[0, i // 2 * 2 + v, i % 2], 1)
     load_block = load(psi_c_hbm, block_of(home_slot), 2)
+
+    def low_or_high(r):
+        return pl.ds(r * (points // 2), points // 2)
 
     def remote(src, dst, send, recv, tile, vec):
         return pltpu.make_async_remote_copy(
@@ -289,19 +297,23 @@
             load(screened_hbm.at[:, columns(turn * 2 + aside)], stage.at[i], 3)
         for i, turn in enumerate(turns):
             load(screened_hbm.at[:, columns(turn * 2 + x)], screened_own.at[i], 4)
-        pltpu.make_async_copy(psi_v_hbm, psi.at[0], local_sem.at[1]).wait()
+        pltpu.make_async_copy(psi.at[0], psi.at[0], local_sem.at[1]).wait()
         ref = psi_half(psi.at[0], half)
         send(ref, psi_half(psi.at[1], half), POINTS, psi_recv.at[0], mate_x, half)
         got(lines(mate_x, half), trial_recv.at[mate_x])
         spread(mate_x, has_up, has_down)
         load_block.wait()
         cross(home_slot, last)
+        along(home_slot, 0, has_up, has_down)
 
         pltpu.make_async_copy(stage, stage, local_sem.at[3]).wait()
         for i in range(slots):
             screened_out[i] = stage[i].astype(bf16)
-        for i in range(slots):
+        for i in range(final):
             send(screened_out.at[i], screened_in.at[i], SHARE, screened_recv.at[i], mate_x, half)
+        for r in range(2):
+            src, dst = screened_out.at[final, low_or_high(r)], screened_in.at[final, low_or_high(r)]
+            send(src, dst, SHARE, screened_recv.at[final + r], mate_x, half)
 
         for e in range(events):
             for xx in range(2):
@@ -310,7 +322,7 @@
                 spread(tile, on_up[e], on_down[e])
             if e == events - 2:
                 cross(home_slot, 0)
-                for s in range(CUTS):
+                for s in range(1, CUTS):
                     if s < CUTS // 2:
                         along(home_slot, s, has_up, has_down)
                     else:
@@ -319,7 +331,7 @@
             for s in range(CUTS // 2, CUTS):
                 along(home_slot, s, has_up & ~at_end, has_down & ~at_end)
         else:
-            for s in range(CUTS):
+            for s in range(1, CUTS):
                 along(home_slot, s, has_up, has_down)
         for s in range(1 if events > 1 else 0, last):
             cross(home_slot, s)
@@ -378,16 +390,26 @@
             if i == turn - 1:
                 arrive(k, CUTS // 2, last)
 
-    def step(p, share, slot, ready=None, done=None):
+    def step(p, share, slot):
         block = block_of(slot)
-        pair = jnp.dot(flat[p], block[...], preferred_element_type=f32)
-        if ready is not None:
-            ready()
-        weighted = (share().astype(f32) * pair).astype(bf16)
+        product = jnp.dot(flat[p], block[...], preferred_element_type=f32)
+        weighted = (share.astype(f32) * product).astype(bf16)
         for h in range(2):
             back[p, h] += back_product(weighted, block[pl.ds(h * middle, middle), :])
-            if done is not None:
-                done(h)
+
+    def last_step():
+        block = block_of(turns[final])
+        pair[...] = jnp.dot(flat[1], block[...], preferred_element_type=f32)
+        for r in range(2):
+            ref = screened_in.at[final, low_or_high(r)]
+            got(ref, screened_recv.at[final + r])
+            weighted = (ref[...].astype(f32) * pair[low_or_high(r)]).astype(bf16)
+            for h in range(2):
+                back[1, h, low_or_high(r)] += back_product(
+                    weighted, block[pl.ds(h * middle, middle), :]
+                )
+                if r == 1:
+                    pl.when(half != h)(functools.partial(swap, 1))
 
     pltpu.make_async_copy(screened_own, screened_own, local_sem.at[4]).wait()
 
@@ -396,18 +418,17 @@
         for i in range(final):
             slot = jnp.where(k == i, turns[i], slot)
             pl.when(k == i)(functools.partial(receive, i))
-        step(0, lambda: screened_own[k], slot)
+        step(0, screened_own[k], slot)
         for i in range(final):
             pl.when(k == i)(functools.partial(between, i))
         got(screened_in.at[k], screened_recv.at[k])
-        step(1, lambda: screened_in[k], slot)
+        step(1, screened_in[k], slot)
         return carry
 
-    final = slots - 1
     with jax.named_scope("puse"):
         lax.fori_loop(0, final, use, 0)
         receive(final)
-        step(0, lambda: screened_own[final], turns[final])
+        step(0, screened_own[final], turns[final])
 
     def span(kind):
         return pl.ds(kind * part, part)
@@ -425,56 +446,51 @@
         low = (total - high.astype(f32)).astype(bf16)
         flat[p, :, pl.ds(middle + kind * part, part)] = low
 
-    block_rows = 2 * rows
-
     def product(p, kind, i):
-        left = psi[p, i].reshape(4 * block_rows, points)
+        left = psi[p, i].reshape(8 * rows, points)
         total = None
         for level in range(2):
             cols = pl.ds(level * middle + kind * part, part)
             value = jnp.dot(left, flat[p, :, cols], preferred_element_type=f32)
             total = value if total is None else total + value
-        return total.reshape(2, 2, block_rows, part)
-
-    def prepare(i):
-        for kind in range(2):
-            if i < AHEAD:
-                keep[kind, i] += product(1, kind, i)
-            else:
-                keep[kind, i] = product(0, kind, i) + product(1, kind, i)
-        for kind in range(2):
-            if kind == 0:
-                away = keep[kind, i, :, pl.ds(aside, 1)]
-            else:
-                away = keep[kind, i, pl.ds(across, 1)]
-            first_send[kind, i] = away.reshape(2, block_rows, part).astype(bf16)
-
-    def leave(i):
-        for kind in range(2):
-            ref = first_send.at[kind, i]
-            recv = first_recv.at[kind, i]
-            send(ref, first_got.at[kind, i], FIRST, recv, [mate_x, mate_y][kind], half)
+        return total.reshape(2, 2, 2, rows, part)
+
+    def prepare(i, kind):
+        if i < AHEAD:
+            keep[kind, i] += product(1, kind, i)
+        else:
+            keep[kind, i] = product(0, kind, i) + product(1, kind, i)
+        if kind == 0:
+            away = keep[kind, i, :, :, pl.ds(aside, 1)]
+        else:
+            away = keep[kind, i, :, pl.ds(across, 1)]
+        first_send[kind, i] = away.reshape(2, 2, rows, part).astype(bf16)
+
+    def leave(i, kind):
+        ref = first_send.at[kind, i]
+        recv = first_recv.at[kind, i]
+        send(ref, first_got.at[kind, i], FIRST, recv, [mate_x, mate_y][kind], half)
 
     def again(i, kind):
         got(first_got.at[kind, i], first_recv.at[kind, i])
         yy, xx = [(across, x), (y, aside)][kind]
-        away = [across, aside][kind]
-        value = keep[kind, i, yy, xx] + first_got[kind, i, away].astype(f32)
+        away, home = [(across, y), (aside, x)][kind]
+        value = keep[kind, i, :, yy, xx] + first_got[kind, i, :, away].astype(f32)
         second_send[kind, i] = value.astype(bf16)
         ref = second_send.at[kind, i]
         recv = second_recv.at[kind, i]
         send(ref, second_got.at[kind, i], SECOND, recv, [mate_y, mate_x][kind], half)
-        keep[kind, i, y, x] += first_got[kind, i, [y, x][kind]].astype(f32)
+        final_sum[kind, i] = keep[kind, i, :, y, x] + first_got[kind, i, :, home].astype(f32)
 
     def deliver(i, kind):
         got(second_got.at[kind, i], second_recv.at[kind, i])
-        value = keep[kind, i, y, x] + second_got[kind, i].astype(f32)
-        keep[kind, i, y, x] = value
+        value = final_sum[kind, i] + second_got[kind, i].astype(f32)
+        final_sum[kind, i] = value
         third[kind, i] = value.astype(bf16)
-        layer = ranks[i]
-        for v in range(2):
+        for side in range(2):
+            layer, v = ranks[i // 2 * 2 + side], i % 2
             send(
-                third.at[kind, i, pl.ds(v * rows, rows)],
+                third.at[kind, i, side],
                 parts.at[half, kind, z],
                 THIRD,
                 parts_recv.at[half, kind],
@@ -493,13 +509,7 @@
     with jax.named_scope("plast"):
         swap(0)
         pl.when(half == 0)(early)
-        step(
-            1,
-            lambda: screened_in[final],
-            turns[final],
-            lambda: got(screened_in.at[final], screened_recv.at[final]),
-            lambda h: pl.when(half != h)(functools.partial(swap, 1)),
-        )
+        last_step()
 
     with jax.named_scope("pearly"):
         pl.when(half == 1)(early)
@@ -507,16 +517,21 @@
     with jax.named_scope("preduce"):
         for kind in range(2):
             split(kind, 1)
+            prepare(0, kind)
+            leave(0, kind)
         lead = layers - 1
-        for i in range(lead):
-            prepare(i)
-            leave(i)
-        prepare(lead)
+        for i in range(1, layers):
+            for kind in range(2):
+                prepare(i, kind)
+            if i < lead:
+                for kind in range(2):
+                    leave(i, kind)
         for i in range(layers):
             for kind in range(2):
                 again(i, kind)
             if i == 0:
-                leave(lead)
+                for kind in range(2):
+                    leave(lead, kind)
             if i > 0:
                 for kind in range(2):
                     deliver(i - 1, kind)
@@ -529,8 +544,8 @@
             for kind in range(2):
                 value = None
                 if flip == 0:
-                    mine = pl.ds(pl.multiple_of(half * rows, rows), rows)
-                    value = keep[kind, place_of(z), y, x, mine]
+                    place = place_of(z)
+                    value = final_sum[kind, (place // 2) * 2 + half, place % 2]
                 count = layers - 1 + flip
                 got(parts.at[vec, kind, pl.ds(0, count)], parts_recv.at[vec, kind])
                 for d in range(1 - flip, layers):
@@ -587,7 +602,7 @@
         out_specs=pl.BlockSpec(memory_space=vmem),
         scratch_shapes=[
             vmem((valence, conduct), bf16),
-            vmem((2, layers, 2, 2, 2 * rows, points), bf16),
+            vmem((2, layers, 2, 2, 2, rows, points), bf16),
             vmem((2, points, valence), bf16),
             vmem((slots, points, width), f32),
             vmem((slots, points, width), f32),
@@ -595,22 +610,24 @@
             vmem((slots, points, width), bf16),
             vmem((slots * conduct, width), bf16),
             vmem((2, points, conduct), bf16),
+            vmem((points, width), f32),
             vmem((2, 2, points, middle), f32),
             vmem((2, 2, points, part), bf16),
             vmem((2, 2, points, part), bf16),
-            vmem((2, layers, 2, 2 * rows, part), bf16),
-            vmem((2, layers, 2, 2 * rows, part), bf16),
-            vmem((2, layers, 2, 2, 2 * rows, part), f32),
-            vmem((2, layers, 2 * rows, part), bf16),
-            vmem((2, layers, 2 * rows, part), bf16),
-            vmem((2, layers, 2 * rows, part), bf16),
+            vmem((2, layers, 2, 2, rows, part), bf16),
+            vmem((2, layers, 2, 2, rows, part), bf16),
+            vmem((2, layers, 2, 2, 2, rows, part), f32),
+            vmem((2, layers, 2, rows, part), f32),
+            vmem((2, layers, 2, rows, part), bf16),
+            vmem((2, layers, 2, rows, part), bf16),
+            vmem((2, layers, 2, rows, part), bf16),
             vmem((2, 2, layers, rows, part), bf16),
             dma((5,)),
             dma((9,)),
             dma((tiles,)),
             dma((1,)),
             dma((2,)),
-            dma((slots,)),
+            dma((slots + 1,)),
             dma((slots, CUTS)),
             dma((2, 2)),
             dma((2, layers)),
@@ -622,7 +639,7 @@
         ),
     )(
         trial[0],
-        psi_v.reshape(layers, 2, 2, 2 * rows, points),
+        psi_v.reshape(layers, 2, 2, 2, rows, points),
         psi_c[:, 0, :],
         screened,
     )

time: 82 us -> 81.3 us (level)
  Pallas kernels: 81.9 us -> 80.6 us
    pallas_call x1, Pallas kernels: 81.2 us -> 79.9 us  [fused(): pl.pallas_call(functools.partial(body, layers), out_shape=vmem((rows, con...]
where the time goes in v10:
time: 81.3 us; the launch traced here: 80.6 us
  Pallas kernels  80.6 us (99%)
    pallas_call x1, Pallas kernels, fused(): pl.pallas_call(functools.partial(body, layers), out_shape=vmem((rows, con...  79.9 us

profile of v10, /device:TPU:0, one launch (start us, length us, event | category | flops | bytes accessed | tf_op | source)
XLA Modules:
  0.0 80.6 jit_solution(3951363373929823928)
XLA Ops:
  0.0 79.9 %shard_map.46.result = f32[32,1024]{1,0:T(8,128)S(1)} custom-call(bf16[32,1024]{1,0:T(8,128)(2,1)} %bitcast.6, bf16[4,2,2,2,32,512]{5,4,3,2,1,0:T(8,128)(2,1)} %bitcast.4, bf16[1024,256]{1,0:T(8,128)(2,1)} %bitcast.5, f32[512,4096]{1,0:T(8,128)} %screened_hbm.1), custom_call_target="tpu_custom_call" | custom-call | tf_op jit(solution)/shard_map/pallas_call | solution.py:598
  80.0 0.7 shard_map.47

commit v11 on v10

--- a/solution.py
+++ b/solution.py
@@ -436,6 +436,7 @@
     def swap(p):
         for kind in range(2):
             give[kind, p] = back[p, other, :, span(kind)].astype(bf16)
+        for kind in range(2):
             send(give.at[kind, p], take.at[kind, p], GIVE, take_recv.at[kind, p], me, other)
 
     def split(kind, p):
@@ -477,16 +478,16 @@
         away, home = [(across, y), (aside, x)][kind]
         value = keep[kind, i, :, yy, xx] + first_got[kind, i, :, away].astype(f32)
         second_send[kind, i] = value.astype(bf16)
+        final_sum[kind, i] = keep[kind, i, :, y, x] + first_got[kind, i, :, home].astype(f32)
         ref = second_send.at[kind, i]
         recv = second_recv.at[kind, i]
         send(ref, second_got.at[kind, i], SECOND, recv, [mate_y, mate_x][kind], half)
-        final_sum[kind, i] = keep[kind, i, :, y, x] + first_got[kind, i, :, home].astype(f32)
 
     def deliver(i, kind):
         got(second_got.at[kind, i], second_recv.at[kind, i])
         value = final_sum[kind, i] + second_got[kind, i].astype(f32)
+        third[kind, i] = value.astype(bf16)
         final_sum[kind, i] = value
-        third[kind, i] = value.astype(bf16)
         for side in range(2):
             layer, v = ranks[i // 2 * 2 + side], i % 2
             send(

time: 81.3 us -> 81.5 us (level)
  no operation moved by 1% of the time
where the time goes in v11:
time: 81.5 us; the launch traced here: 80.7 us
  Pallas kernels  80.7 us (99%)
    pallas_call x1, Pallas kernels, fused(): pl.pallas_call(functools.partial(body, layers), out_shape=vmem((rows, con...  80 us

profile of v11, /device:TPU:0, one launch (start us, length us, event | category | flops | bytes accessed | tf_op | source)
XLA Modules:
  0.0 80.7 jit_solution(6144983009995696014)
XLA Ops:
  0.0 80.0 %shard_map.46.result = f32[32,1024]{1,0:T(8,128)S(1)} custom-call(bf16[32,1024]{1,0:T(8,128)(2,1)} %bitcast.6, bf16[4,2,2,2,32,512]{5,4,3,2,1,0:T(8,128)(2,1)} %bitcast.4, bf16[1024,256]{1,0:T(8,128)(2,1)} %bitcast.5, f32[512,4096]{1,0:T(8,128)} %screened_hbm.1), custom_call_target="tpu_custom_call" | custom-call | tf_op jit(solution)/shard_map/pallas_call | solution.py:599
  80.1 0.7 shard_map.47

commit v12 on v10

--- a/solution.py
+++ b/solution.py
@@ -99,10 +99,12 @@
     local_sem,
     sends,
     trial_recv,
+    across_recv,
     hand_recv,
     psi_recv,
     screened_recv,
     block_recv,
+    mate_recv,
     take_recv,
     first_recv,
     second_recv,
@@ -237,28 +239,34 @@
         ref = lines(tile, half)
         send(ref, ref, ROWS, hand_recv.at[0], me, other)
 
+    def rows_sem(tile):
+        return trial_recv.at[(tile // 4) * 2 + tile % 2]
+
     def spread(tile, to_up, to_down):
         ref = lines(tile, half)
-        recv = trial_recv.at[tile]
+        recv = rows_sem(tile)
         send(ref, ref, ROWS, recv, tile_of(up, y, x), half, to_up)
         send(ref, ref, ROWS, recv, tile_of(down, y, x), half, to_down)
-        send(ref, ref, ROWS, recv, mate_y, half)
+        send(ref, ref, ROWS, across_recv.at[0], mate_y, half)
         hand(tile)
 
     last = CUTS - 1
 
-    def along(slot, s, to_up, to_down):
+    def along(slot, s, to_up, to_down, mate=False):
         ref = piece(slot, s)
-        recv = block_recv.at[slot, s]
+        recv = mate_recv.at[slot // 2, 1] if mate else block_recv.at[slot // 2, s]
         send(ref, ref, LAYERS, recv, tile_of(up, y, x), half, to_up)
         send(ref, ref, LAYERS, recv, tile_of(down, y, x), half, to_down)
 
     def cross(slot, s):
         ref = piece(slot, s)
-        send(ref, ref, ACROSS, block_recv.at[slot, s], mate_y, half)
+        send(ref, ref, ACROSS, mate_recv.at[slot // 2, s // last], mate_y, half)
 
     def came(slot, s):
-        got(piece(slot, s), block_recv.at[slot, s])
+        got(piece(slot, s), block_recv.at[slot // 2, s])
+
+    def mate_came(slot):
+        got(piece(slot, last), mate_recv.at[slot // 2, 1])
 
     pair_layers = layers // 2
 
@@ -274,8 +282,8 @@
 
     def take_mate(e):
         slot = slot_of(source[e], across)
-        came(slot, last)
-        along(slot, last, on_up[e], on_down[e])
+        mate_came(slot)
+        along(slot, last, on_up[e], on_down[e], True)
 
     def at_k(k):
         return [e for e in range(events) if any(abs(row[e] - r) == k for r, row in enumerate(table))]
@@ -291,7 +299,7 @@
     with jax.named_scope("ptrial"):
         ref = lines(me, half)
         load_rows.wait()
-        send(ref, ref, ROWS, trial_recv.at[me], mate_x, half)
+        send(ref, ref, ROWS, rows_sem(me), mate_x, half)
         spread(me, has_up, has_down)
         for i, turn in enumerate(turns):
             load(screened_hbm.at[:, columns(turn * 2 + aside)], stage.at[i], 3)
@@ -300,7 +308,7 @@
         pltpu.make_async_copy(psi.at[0], psi.at[0], local_sem.at[1]).wait()
         ref = psi_half(psi.at[0], half)
         send(ref, psi_half(psi.at[1], half), POINTS, psi_recv.at[0], mate_x, half)
-        got(lines(mate_x, half), trial_recv.at[mate_x])
+        got(lines(mate_x, half), rows_sem(mate_x))
         spread(mate_x, has_up, has_down)
         load_block.wait()
         cross(home_slot, last)
@@ -318,7 +326,7 @@
         for e in range(events):
             for xx in range(2):
                 tile = tile_of(source[e], y, xx)
-                got(lines(tile, half), trial_recv.at[tile])
+                got(lines(tile, half), rows_sem(tile))
                 spread(tile, on_up[e], on_down[e])
             if e == events - 2:
                 cross(home_slot, 0)
@@ -340,14 +348,13 @@
         valence = layers * 4 * 2 * rows
         psi_t[0] = psi[0].reshape(valence, points).T
 
-        came(mate_slot, last)
-        along(mate_slot, last, has_up, has_down)
+        mate_came(mate_slot)
+        along(mate_slot, last, has_up, has_down, True)
         arrive(1, 0, CUTS // 2)
+        got(whole.at[pl.ds(0, layers * 2 * rows), :], across_recv.at[0])
         for e in range(-1, events):
             for xx in range(2):
-                tile = tile_of(source[e] if e >= 0 else z, across, xx)
-                got(lines(tile, half), trial_recv.at[tile])
-                hand(tile)
+                hand(tile_of(source[e] if e >= 0 else z, across, xx))
 
         ref = psi_half(psi.at[1], half)
         got(ref, psi_recv.at[0])
@@ -380,8 +387,8 @@
         if kind == "z" and e > 0:
             arrive(e + 1, last, CUTS)
         if kind == "y":
-            for s in range(last):
-                came(turns[i], s)
+            start = pl.multiple_of(turns[i] * conduct, conduct)
+            got(panel.at[pl.ds(start, last * height), :], mate_recv.at[turns[i] // 2, 0])
 
     def between(i):
         for k, turn in turn_of.items():
@@ -578,9 +585,11 @@
 
 
 def write_out(result, out_hbm, sem):
-    copy = pltpu.make_async_copy(result, out_hbm, sem)
-    copy.start()
-    copy.wait()
+    part = result.shape[1] // 4
+    for i in range(4):
+        lot = pl.ds(i * part, part)
+        pltpu.make_async_copy(result.at[:, lot], out_hbm.at[:, lot], sem).start()
+    pltpu.make_async_copy(result, out_hbm, sem).wait()
 
 
 def fused(tiles, trial, psi_v, psi_c, screened):
@@ -624,11 +633,13 @@
             vmem((2, 2, layers, rows, part), bf16),
             dma((5,)),
             dma((9,)),
-            dma((tiles,)),
+            dma((slots,)),
+            dma((1,)),
             dma((1,)),
             dma((2,)),
             dma((slots + 1,)),
-            dma((slots, CUTS)),
+            dma((layers, CUTS)),
+            dma((layers, 2)),
             dma((2, 2)),
             dma((2, layers)),
             dma((2, layers)),

time: 81.3 us -> 81.1 us (level)
  no operation moved by 1% of the time
where the time goes in v12:
time: 81.1 us; the launch traced here: 80.5 us
  Pallas kernels  80.5 us (99%)
    pallas_call x1, Pallas kernels, fused(): pl.pallas_call(functools.partial(body, layers), out_shape=vmem((rows, con...  79.8 us

profile of v12, /device:TPU:0, one launch (start us, length us, event | category | flops | bytes accessed | tf_op | source)
XLA Modules:
  0.0 80.5 jit_solution(8088843607657475400)
XLA Ops:
  0.0 79.8 %shard_map.46.result = f32[32,1024]{1,0:T(8,128)S(1)} custom-call(bf16[32,1024]{1,0:T(8,128)(2,1)} %bitcast.6, bf16[4,2,2,2,32,512]{5,4,3,2,1,0:T(8,128)(2,1)} %bitcast.4, bf16[1024,256]{1,0:T(8,128)(2,1)} %bitcast.5, f32[512,4096]{1,0:T(8,128)} %screened_hbm.1), custom_call_target="tpu_custom_call" | custom-call | tf_op jit(solution)/shard_map/pallas_call | solution.py:607
  79.8 0.7 shard_map.47
